TPU v7x, 512 devices: a whole 4x8x8 slice. The times are simulated.
512 devices in a mesh: layer: 4 (over x), feat: 32 (over z, y_lo), width: 4 (over y_hi, core).
Axes of the slice: x: 4, y: 8 (y_hi: 2, y_lo: 4; y = y_hi * 4 + y_lo), z: 8, core: 2. Of those that a mesh axis runs over, the one named last changes fastest.
Arguments:
- residuals: bfloat16 [4, 1024, 2304], P('layer', 'feat', 'width'), may hold values from -6 to 6
- cotangent: bfloat16 [4, 1024, 2304], P('layer', 'feat', 'width'), may hold values from -6 to 6
- enc_weight: bfloat16 [4, 2304, 8192], P('layer', 'width', 'feat'), may hold values from -0.125 to 0.125
- enc_bias: float32 [4, 8192], P('layer', 'feat'), may hold values from -3 to 3
- dec_weight: bfloat16 [4, 4, 8192, 2304], P('layer', None, 'feat', 'width'), may hold values from -0.0625 to 0.0625
- active: int32 [4, 1024, 8192], P('layer', None, 'feat'), may hold values 0 or 1
Outputs:
- dec_grad: bfloat16 [4, 4, 8192, 2304], P('layer', None, 'feat', 'width')
- enc_grad: bfloat16 [4, 2304, 8192], P('layer', 'width', 'feat')
- bias_grad: float32 [4, 8192], P('layer', 'feat')
- feat_grad: bfloat16 [4, 1024, 8192], P('layer', None, 'feat')
All inputs are finite; a program needn't handle non-finite values. No bound on the sum of `active` on one device may be relied on, other than what follows from the above.
Results may differ from a plain program's by a relative error of at most 0.005.
Values may be sent and summed in bfloat16 or wider, within the bound.
A program may use at most 64 MiB of HBM per device.

v0:
```python
import jax
import jax.numpy as jnp
from jax import lax
from jax.sharding import PartitionSpec as P


def local(residuals, cotangent, enc_weight, enc_bias, dec_weight, active):
    layers = dec_weight.shape[1]
    source = lax.axis_index("layer")
    local_grads = lax.all_gather(cotangent, "layer", axis=0, tiled=True)
    whole_resid, whole_grads = (
        lax.all_gather(residuals[0], "feat", axis=0, tiled=True),
        lax.all_gather(local_grads, "feat", axis=1, tiled=True),
    )
    later_mask = (jnp.arange(layers) >= source)[:, None, None]
    used_grads = jnp.where(later_mask, whole_grads, jnp.zeros_like(whole_grads))
    enc_part = jnp.dot(whole_resid, enc_weight[0], preferred_element_type=jnp.float32)
    feat_part = jnp.einsum(
        "ktd,kfd->tf", used_grads, dec_weight[0], preferred_element_type=jnp.float32
    )
    enc_total, feat_total = lax.psum((enc_part, feat_part), "width")
    gate_all = active[0].astype(jnp.float32)
    activation = ((enc_total + enc_bias) * gate_all).astype(jnp.bfloat16)
    feat_grad = (feat_total * gate_all).astype(jnp.bfloat16)
    dec_grad = jnp.einsum(
        "tf,ktd->kfd", activation, used_grads, preferred_element_type=jnp.float32
    ).astype(jnp.bfloat16)
    enc_grad = lax.dot_general(
        whole_resid, feat_grad, (((0,), (0,)), ((), ())), preferred_element_type=jnp.float32
    ).astype(jnp.bfloat16)
    bias_grad = jnp.sum(feat_grad, axis=0, dtype=jnp.float32)
    return (dec_grad[None], enc_grad[None], bias_grad[None], feat_grad[None])


def solution(mesh):
    in_specs = (
        P("layer", "feat", "width"),
        P("layer", "feat", "width"),
        P("layer", "width", "feat"),
        P("layer", "feat"),
        P("layer", None, "feat", "width"),
        P("layer", None, "feat"),
    )
    out_specs = (
        P("layer", None, "feat", "width"),
        P("layer", "width", "feat"),
        P("layer", "feat"),
        P("layer", None, "feat"),
    )
    return jax.shard_map(local, mesh=mesh, in_specs=in_specs, out_specs=out_specs, check_vma=False)
```

profile of v0, /device:TPU:1, one launch (start us, length us, event | category | flops | bytes accessed | tf_op | source)
XLA Modules:
  0.0 466.8 jit_solution(9379940428828128747)
XLA Ops:
  7.2 0.0 copy-start
  7.2 0.0 all-gather.6.cloned.1.call-start
  7.2 0.7 all-gather.6.cloned.1.call-update
  7.9 0.0 all-gather.4.cloned.1.call-start
  8.0 12.6 %all_gather.9 = bf16[4,32,576]{2,1,0:T(8,128)(2,1)} all-gather(bf16[1,32,576]{2,1,0:T(8,128)(2,1)} %param.7), channel_id=1, replica_groups=mesh['layer'=4,'feat'=32,'width'=4] {'layer'}, dimensions={0}, use_global_device_ids=true | all-gather | bytes 184320 | tf_op jit(solution)/shard_map/all_gather | solution.py:10
  20.5 0.0 all-gather.4.cloned.1.call-update
  20.6 0.0 all-reduce.3.cloned.1.call-start
  20.6 127.4 %all-gather.6.cloned.1.call-done = bf16[1,1024,576]{2,1,0:T(8,128)(2,1)} async-done(((bf16[1,32,576]{2,1,0:T(8,128)(2,1)}), bf16[1,1024,576]{2,1,0:T(8,128)(2,1)}) %all-gather.6.cloned.1.call-update) | async-done | bytes 1179664 | tf_op jit(solution)/shard_map/all_gather | solution.py:12
  148.0 2.9 fusion.7
  150.9 171.4 %all-gather.4.cloned.1.call-done = bf16[4,1024,576]{2,1,0:T(8,128)(2,1)} async-done(((bf16[4,32,576]{2,1,0:T(8,128)(2,1)}), bf16[4,1024,576]{2,1,0:T(8,128)(2,1)}) %all-gather.4.cloned.1.call-update) | async-done | bytes 4718608 | tf_op jit(solution)/shard_map/all_gather | solution.py:13
  322.3 0.0 copy-done
  322.3 5.2 %fusion.4 = f32[1024,256]{1,0:T(8,128)} fusion(bf16[4,1024,576]{2,1,0:T(8,128)(2,1)} %all-gather.4.cloned.1.call-done, pred[4]{0:T(512)(128)(4,1)S(1)} %iota_compare_fusion, bf16[1,4,256,576]{2,3,1,0:T(8,128)(2,1)S(1)} %copy-done), kind=kOutput, calls=%fused_computation.5 | convolution fusion | flops 1210318848 | bytes 6946820 | tf_op jit(solution)/shard_map/ktd,kfd->tf/dot_general | solution.py:18
  327.4 0.0 copy-start.3
  327.4 0.0 copy-start.1
  327.4 0.0 all-reduce.3.cloned.1.call-update
  327.5 124.2 %all-reduce.3.cloned.1.call-done = (f32[1024,256]{1,0:T(8,128)}, f32[1024,256]{1,0:T(8,128)}) async-done(((f32[1024,256]{1,0:T(8,128)}, f32[1024,256]{1,0:T(8,128)}), (f32[1024,256]{1,0:T(8,128)}, f32[1024,256]{1,0:T(8,128)})) %all-reduce.3.cloned.1.call-update) | async-done | bytes 2097168 | tf_op jit(solution)/shard_map/psum | solution.py:21
  451.7 0.0 copy-done.3
  451.7 0.0 copy-start.4
  451.7 0.0 copy-start.5
  451.7 2.1 convert_reduce_fusion
  453.8 0.0 copy-start.2
  453.8 0.0 copy-done.1
  453.8 1.3 fusion.13
  455.1 0.0 copy-done.4
  455.1 0.0 copy-done.5
  455.1 5.2 %fusion.3 = bf16[1,4,256,576]{2,3,1,0:T(8,128)(2,1)} fusion(bf16[4,1024,576]{2,1,0:T(8,128)(2,1)} %all-gather.4.cloned.1.call-done, pred[4]{0:T(512)(128)(4,1)S(1)} %iota_compare_fusion, s32[1,1024,256]{2,1,0:T(8,128)S(1)} %copy-done.3, f32[1024,256]{1,0:T(8,128)S(1)} %copy-done.4, f32[256]{0:T(256)S(1)} %bitcast.45), kind=kOutput, calls=%fused_computation.4 | convolution fusion | flops 1211957248 | bytes 7996420 | tf_op jit(solution)/shard_map/tf,ktd->kfd/dot_general | solution.py:25
  460.3 0.0 copy-done.2
  (1 shorter events, 0.0 us)
Async XLA Ops:
  7.2 315.1 %copy-start = (bf16[1,4,256,576]{2,3,1,0:T(8,128)(2,1)S(1)}, bf16[1,4,256,576]{2,3,1,0:T(8,128)(2,1)}, u32[]{:S(2)}) copy-start(bf16[1,4,256,576]{2,3,1,0:T(8,128)(2,1)} %param.10) | copy-start | bytes 3538948
  7.2 140.8 %all-gather.6.cloned.1.call-start = ((), (), s32[]{:S(2)}) async-start(), calls=%async_computation.1 | async-start | bytes 1351680 | tf_op jit(solution)/shard_map/all_gather | solution.py:12
  7.9 314.4 %all-gather.4.cloned.1.call-start = ((), (), s32[]{:S(2)}) async-start(), calls=%async_computation | async-start | bytes 5406720 | tf_op jit(solution)/shard_map/all_gather | solution.py:13
  20.6 431.1 %all-reduce.3.cloned.1.call-start = ((), (), s32[]{:S(2)}) async-start(), calls=%async_computation.2 | async-start | bytes 4194304 | tf_op jit(solution)/shard_map/psum | solution.py:21
  327.4 124.2 %copy-start.3 = (s32[1,1024,256]{2,1,0:T(8,128)S(1)}, s32[1,1024,256]{2,1,0:T(8,128)}, u32[]{:S(2)}) copy-start(s32[1,1024,256]{2,1,0:T(8,128)} %param.11) | copy-start | bytes 3145732
  327.4 126.3 %copy-start.1 = (bf16[1,1024,576]{2,1,0:T(8,128)(2,1)S(1)}, bf16[1,1024,576]{2,1,0:T(8,128)(2,1)}, u32[]{:S(2)}) copy-start(bf16[1,1024,576]{2,1,0:T(8,128)(2,1)} %all-gather.6.cloned.1.call-done) | copy-start | bytes 3538948
  451.7 3.4 copy-start.4
  451.7 3.4 copy-start.5
  453.8 6.5 %copy-start.2 = (bf16[1024,256]{1,0:T(8,128)(2,1)}, bf16[1024,256]{1,0:T(8,128)(2,1)S(1)}, u32[]{:S(2)}) copy-start(bf16[1024,256]{1,0:T(8,128)(2,1)S(1)} %get-tuple-element.7) | copy-start | bytes 1572868
Sparse Core Ops, SparseCore 0:
  10.1 137.8 all-gather.5
  150.1 172.1 all-gather.3
  327.6 124.0 all-reduce.2
where the time goes:
time: 467 us
  waiting for transfers between devices  424 us (91%)
  matrix products  14.6 us (3%)
  between operations  13.8 us (3%)
  blocking collectives  12.6 us (3%)
    all_gather x1, waiting for transfers between devices, local(): lax.all_gather(local_grads, 'feat', axis=1, tiled=True)  171 us
    all_gather x1, waiting for transfers between devices, local(): lax.all_gather(residuals[0], 'feat', axis=0, tiled=True)  127 us
    psum x1, waiting for transfers between devices, local(): enc_total, feat_total = lax.psum((enc_part, feat_part), 'width')  124 us
    all_gather x1, blocking collectives, local(): local_grads = lax.all_gather(cotangent, 'layer', axis=0, tiled=True)  12.6 us
  transfers between devices with their start and end apart: 3, of which 3 were waited for; matrix products, arithmetic and copies ran while one was open for 1% of the time, Pallas kernels for 0%

commit v1 on v0

v1 whole, which is shorter than its diff:
```python
import jax
import jax.numpy as jnp
from jax import lax
from jax.experimental import pallas as pl
from jax.experimental.pallas import tpu as pltpu
from jax.sharding import PartitionSpec as P

MESH = pl.DeviceIdType.MESH
BF16, F32 = jnp.bfloat16, jnp.float32

NX, NZ, NJ = 4, 8, 4
TOK = 32
ROWS = NJ * TOK
HALF = ROWS // 2
D = 576
PAD = 640
OFF = PAD - D
FEATS = 256
T_HOPS = 2


def nt(a, b):
    return lax.dot_general(a, b, (((1,), (1,)), ((), ())), preferred_element_type=F32)


def tn(a, b):
    return lax.dot_general(a, b, (((0,), (0,)), ((), ())), preferred_element_type=F32)


def kernel(
    resid, cot, bias, encw_hbm, decw_hbm, active_hbm,
    dec_out, enc_out, bias_out, fg_out,
    gp, cots, encw, ew, decw, dw, active,
    part, r1, s2, r2, af,
    loc_sem, p_recv, c_recv, zp_send, zt_send, yp_send, yt_send, xs_send, tx_send,
    r_recv, r_send,
):
    x = lax.axis_index("layer")
    f = lax.axis_index("feat")
    w = lax.axis_index("width")
    z, j = lax.div(f, NJ), lax.rem(f, NJ)
    c = lax.rem(w, 2)

    def at(dx=0, zz=None, jj=None, ww=None):
        zz = z if zz is None else zz
        jj = j if jj is None else jj
        return {"layer": lax.rem(x + dx, NX), "feat": zz * NJ + jj, "width": w if ww is None else ww}

    zi = lambda d: lax.rem(z + d + NZ, NZ)
    up, down = at(zz=zi(1)), at(zz=zi(-1))
    core_peer = at(ww=w + 1 - 2 * c)
    far_peer = at(ww=lax.rem(w + 2, 4))
    y_next, y_prev = at(jj=j + 1), at(jj=j - 1)
    o1 = jnp.where(j == 0, 1, j - 1)
    o2 = jnp.where(j == 0, 2, jnp.where(j == 3, 1, j + 1))
    o3 = jnp.where(j < 2, 3, 0)
    order = [j, o1, o2, o3]

    loads = [
        (pltpu.make_async_copy(encw_hbm.at[0], encw, loc_sem.at[4]), None),
        (pltpu.make_async_copy(active_hbm.at[0], active, loc_sem.at[5]), None),
    ]
    for k in range(NX):
        loads.append((pltpu.make_async_copy(decw_hbm.at[0, jnp.minimum(x + k, NX - 1)], decw.at[k], loc_sem.at[k]), x + k < NX))
    for cp, cond in loads:
        if cond is None:
            cp.start()
        else:
            pl.when(cond)(cp.start)

    barrier = pltpu.get_barrier_semaphore()

    def greet(dev):
        pl.semaphore_signal(barrier, inc=1, device_id=dev, device_id_type=MESH)

    for dev in (core_peer, far_peer, up, down, at(1), at(2), at(3)):
        greet(dev)
    pl.when(j < NJ - 1)(lambda: greet(y_next))
    pl.when(j > 0)(lambda: greet(y_prev))
    gp[f] = jnp.concatenate([resid[0], cot[0]], axis=1)
    pl.semaphore_wait(barrier, 7 + (j > 0).astype(jnp.int32) + (j < NJ - 1).astype(jnp.int32))

    def remote(src, dst, ss, rs, dev):
        return pltpu.make_async_remote_copy(src, dst, ss, rs, device_id=dev, device_id_type=MESH)

    sent = []

    def send(cp, cond=None):
        sent.append((cp, cond))
        if cond is None:
            cp.start()
        else:
            pl.when(cond)(cp.start)

    own_cot = lambda fi: gp.at[fi, :, pl.ds(2 * D - PAD, PAD)]

    def send_z(fi, d, cond=None):
        send(remote(gp.at[fi], gp.at[fi], zp_send.at[d, fi], p_recv.at[fi], (up, down)[d]), cond)

    def send_zt(fi, d, cond):
        send(remote(cots.at[1, fi], cots.at[1, fi], zt_send.at[d, fi], c_recv.at[1, fi], (up, down)[d]), cond)

    def send_x(fi):
        send(remote(own_cot(fi), cots.at[0, fi], xs_send.at[0, fi], c_recv.at[0, fi], at(3)), x >= 1)
        send(remote(own_cot(fi), cots.at[2, fi], xs_send.at[1, fi], c_recv.at[2, fi], at(1)), x == 3)

    def wait_p(fi):
        remote(gp.at[fi], gp.at[fi], zp_send.at[0, fi], p_recv.at[fi], up).wait_recv()

    def wait_c(k, fi):
        remote(cots.at[k, fi], cots.at[k, fi], zp_send.at[0, fi], c_recv.at[k, fi], up).wait_recv()

    for d in (0, 1):
        send_z(f, d)
    send(remote(gp.at[f], gp.at[f], yp_send.at[0, j], p_recv.at[f], y_next), j < NJ - 1)
    send(remote(gp.at[f], gp.at[f], yp_send.at[1, j], p_recv.at[f], y_prev), j > 0)
    send(remote(own_cot(f), cots.at[1, f], tx_send.at[f], c_recv.at[1, f], at(2)), x >= 2)
    send_x(f)

    third = x <= 1

    def ev_t_own():
        pl.when(third)(lambda: wait_c(1, f))
        for d in (0, 1):
            send_zt(f, d, third)
        send(remote(cots.at[1, f], cots.at[1, f], yt_send.at[0, j], c_recv.at[1, f], y_next), third & (j < NJ - 1))
        send(remote(cots.at[1, f], cots.at[1, f], yt_send.at[1, j], c_recv.at[1, f], y_prev), third & (j > 0))

    def ev_y(i):
        oi = order[i]
        fi = z * NJ + oi
        wait_p(fi)
        send(remote(gp.at[fi], gp.at[fi], yp_send.at[0, oi], p_recv.at[fi], y_next), (oi < j) & (j < NJ - 1))
        send(remote(gp.at[fi], gp.at[fi], yp_send.at[1, oi], p_recv.at[fi], y_prev), (oi > j) & (j > 0))
        for d in (0, 1):
            send_z(fi, d)
        send_x(fi)

    def ev_yt(i):
        oi = order[i]
        fi = z * NJ + oi
        pl.when(third)(lambda: wait_c(1, fi))
        send(remote(cots.at[1, fi], cots.at[1, fi], yt_send.at[0, oi], c_recv.at[1, fi], y_next), third & (oi < j) & (j < NJ - 1))
        send(remote(cots.at[1, fi], cots.at[1, fi], yt_send.at[1, oi], c_recv.at[1, fi], y_prev), third & (oi > j) & (j > 0))
        for d in (0, 1):
            send_zt(fi, d, third)

    def ev_z(r, i, d):
        fi = zi(-r if d == 0 else r) * NJ + order[i]
        wait_p(fi)
        if r < 3 or (r == 3 and (i < 2) == (d == 0)):
            send_z(fi, d)
        send_x(fi)

    def ev_zt(r, i, d):
        fi = zi(-r if d == 0 else r) * NJ + order[i]
        pl.when(third)(lambda: wait_c(1, fi))
        if r < T_HOPS:
            send_zt(fi, d, third)

    relay = (x == 1) | (x == 2)
    waited_a = set()

    def ev_relay(r, i, sgn):
        fi = zi(sgn * r) * NJ + order[i]
        pl.when(relay)(lambda: wait_c(0, fi))
        send(remote(cots.at[0, fi], cots.at[1, fi], tx_send.at[fi], c_recv.at[1, fi], at(3)), relay)

    def setup():
        for cp, cond in loads:
            if cond is None:
                cp.wait()
            else:
                pl.when(cond)(cp.wait)
        ew[0:D, :] = encw[...]
        ew[D:PAD, :] = jnp.zeros((OFF, FEATS), BF16)
        for k in range(NX):
            @pl.when(x + k < NX)
            def _():
                dw[k] = jnp.concatenate([jnp.zeros((FEATS, OFF), BF16), decw[k]], axis=1)

    def block(zz):
        rows = gp.at[pl.ds(zz * NJ, NJ)]
        part[zz, 0] = jnp.dot(rows[:, :, 0:PAD].reshape(ROWS, PAD), ew[...], preferred_element_type=F32)
        part[zz, 1] = nt(rows[:, :, 2 * D - PAD :].reshape(ROWS, PAD), dw[0])

    def block_c(zz, k, cond):
        @pl.when(cond)
        def _():
            part[zz, 1] += nt(cots[k, pl.ds(zz * NJ, NJ)].reshape(ROWS, PAD), dw[k + 1])

    def wait_block(zz, d):
        for i in range(NJ):
            fi = zz * NJ + order[i]
            if abs(d) > T_HOPS:
                pl.when(x == 0)(lambda: wait_c(0, fi))
                pl.when(third)(lambda: wait_c(1, fi))
            else:
                pl.when(x <= 2)(lambda: wait_c(0, fi))
            pl.when(x == 0)(lambda: wait_c(2, fi))

    mine = pl.ds(pl.multiple_of(c * HALF, HALF), HALF)
    other = pl.ds(pl.multiple_of((1 - c) * HALF, HALF), HALF)

    def red1(zz):
        send(remote(part.at[zz, :, other], r1.at[zz], r_send.at[0, zz], r_recv.at[0, zz], core_peer))

    def red2(zz):
        remote(part.at[zz, :, other], r1.at[zz], r_send.at[0, zz], r_recv.at[0, zz], core_peer).wait_recv()
        s2[zz] = (part[zz, :, mine, :] + r1[zz]).astype(BF16)
        send(remote(s2.at[zz], r2.at[zz], r_send.at[1, zz], r_recv.at[1, zz], far_peer))

    def red3(zz):
        remote(s2.at[zz], r2.at[zz], r_send.at[1, zz], r_recv.at[1, zz], far_peer).wait_recv()
        total = s2[zz].astype(F32) + r2[zz].astype(F32)
        rows = pl.ds(pl.multiple_of(zz * ROWS + c * HALF, HALF), HALF)
        gate = active[rows, :].astype(F32)
        af[0, rows, :] = ((total[0] + bias[...]) * gate).astype(BF16)
        af[1, rows, :] = (total[1] * gate).astype(BF16)
        send(remote(af.at[:, rows], af.at[:, rows], r_send.at[2, zz], r_recv.at[2, zz], core_peer))

    def red4(zz):
        rows = pl.ds(pl.multiple_of(zz * ROWS + (1 - c) * HALF, HALF), HALF)
        remote(af.at[:, rows], af.at[:, rows], r_send.at[2, zz], r_recv.at[2, zz], core_peer).wait_recv()

    def compute(d):
        zz = zi(d)
        wait_block(zz, d)
        block(zz)
        block_c(zz, 0, x <= 2)
        block_c(zz, 1, x <= 1)
        block_c(zz, 2, x == 0)
        red1(zz)

    setup()
    ev_t_own()
    for i in (1, 2, 3):
        ev_y(i)
        ev_yt(i)
    for i in range(NJ):
        for d in (0, 1):
            ev_z(1, i, d)
            ev_zt(1, i, d)
    compute(0)
    for i in range(NJ):
        for d in (0, 1):
            ev_z(2, i, d)
            ev_zt(2, i, d)
    compute(-1)
    compute(1)
    red2(zi(0))
    for i in range(NJ):
        for d in (0, 1):
            ev_z(3, i, d)
    red2(zi(-1))
    red2(zi(1))
    red3(zi(0))
    compute(-2)
    compute(2)
    for i in range(NJ):
        ev_relay(3, i, -1)
        ev_relay(3, i, 1)
    for i in range(NJ):
        ev_z(4, i, 0 if i < 2 else 1)
    for d in (-1, 1):
        red3(zi(d))
    for d in (-2, 2):
        red2(zi(d))
    compute(-3)
    compute(3)
    for d in (-2, 2):
        red3(zi(d))
    for i in range(NJ):
        ev_relay(4, i, 1)
    compute(4)
    for d in (-3, 3, 4):
        red2(zi(d))
    for d in (-3, 3, 4):
        red3(zi(d))
    for d in (0, -1, 1, -2, 2, -3, 3, 4):
        red4(zi(d))

    act = af[0]
    fg = af[1]
    for t in range(NX):
        @pl.when(t < x)
        def _():
            dec_out[0, t] = jnp.zeros((FEATS, D), BF16)

    tokens = NZ * ROWS
    dec_out[0, x] = tn(act, gp[:, :, 2 * D - PAD :].reshape(tokens, PAD))[:, OFF:].astype(BF16)
    for k in range(NX - 1):
        @pl.when(x + k + 1 < NX)
        def _():
            dec_out[0, x + k + 1] = tn(act, cots[k].reshape(tokens, PAD))[:, OFF:].astype(BF16)
    enc_out[0] = tn(gp[:, :, 0:PAD].reshape(tokens, PAD), fg)[0:D, :].astype(BF16)
    bias_out[...] = jnp.sum(fg.astype(F32), axis=0, keepdims=True)
    fg_out[0] = fg

    for cp, cond in sent:
        if cond is None:
            cp.wait_send()
        else:
            pl.when(cond)(cp.wait_send)


def local(residuals, cotangent, enc_weight, enc_bias, dec_weight, active):
    vmem, hbm = pl.BlockSpec(memory_space=pltpu.VMEM), pl.BlockSpec(memory_space=pl.ANY)
    chunks, dma = NZ * NJ, pltpu.SemaphoreType.DMA
    return pl.pallas_call(
        kernel,
        out_shape=(
            jax.ShapeDtypeStruct((1, NX, FEATS, D), BF16),
            jax.ShapeDtypeStruct((1, D, FEATS), BF16),
            jax.ShapeDtypeStruct((1, FEATS), F32),
            jax.ShapeDtypeStruct((1, NZ * ROWS, FEATS), BF16),
        ),
        in_specs=[vmem, vmem, vmem, hbm, hbm, hbm],
        out_specs=(vmem, vmem, vmem, vmem),
        scratch_shapes=[
            pltpu.VMEM((chunks, TOK, 2 * D), BF16),
            pltpu.VMEM((3, chunks, TOK, PAD), BF16),
            pltpu.VMEM((D, FEATS), BF16),
            pltpu.VMEM((PAD, FEATS), BF16),
            pltpu.VMEM((NX, FEATS, D), BF16),
            pltpu.VMEM((NX, FEATS, PAD), BF16),
            pltpu.VMEM((NZ * ROWS, FEATS), jnp.int32),
            pltpu.VMEM((NZ, 2, ROWS, FEATS), F32),
            pltpu.VMEM((NZ, 2, HALF, FEATS), F32),
            pltpu.VMEM((NZ, 2, HALF, FEATS), BF16),
            pltpu.VMEM((NZ, 2, HALF, FEATS), BF16),
            pltpu.VMEM((2, NZ * ROWS, FEATS), BF16),
            dma((6,)),
            dma((chunks,)),
            dma((3, chunks)),
            dma((2, chunks)),
            dma((2, chunks)),
            dma((2, NJ)),
            dma((2, NJ)),
            dma((2, chunks)),
            dma((chunks,)),
            dma((3, NZ)),
            dma((3, NZ)),
        ],
        compiler_params=pltpu.CompilerParams(collective_id=0, has_side_effects=True, vmem_limit_bytes=60 * 2**20),
    )(residuals, cotangent, enc_bias, enc_weight, dec_weight, active)


def solution(mesh):
    in_specs = (
        P("layer", "feat", "width"),
        P("layer", "feat", "width"),
        P("layer", "width", "feat"),
        P("layer", "feat"),
        P("layer", None, "feat", "width"),
        P("layer", None, "feat"),
    )
    out_specs = (
        P("layer", None, "feat", "width"),
        P("layer", "width", "feat"),
        P("layer", "feat"),
        P("layer", None, "feat"),
    )
    return jax.shard_map(local, mesh=mesh, in_specs=in_specs, out_specs=out_specs, check_vma=False)
```

time: 467 us -> 96.9 us (0.21)
  waiting for transfers between devices: 424 us -> 0 us
  Pallas kernels: 0 us -> 89.1 us
  matrix products: 14.6 us -> 0 us
  between operations: 13.8 us -> 0.67 us
  blocking collectives: 12.6 us -> 0 us
  local copies, waits for them, and re-layouts: 0.03 us -> 6.95 us
    all_gather x2 -> x0, waiting for transfers between devices: 299 us -> none  [the longest x1 171 us: local(): lax.all_gather(local_grads, 'feat', axis=1, tiled=True)]
    psum x1 -> x0, waiting for transfers between devices: 124 us -> none  [local(): enc_total, feat_total = lax.psum((enc_part, feat_part), 'width')]
    pallas_call x0 -> x1, Pallas kernels: none -> 89.1 us  [local(): pl.pallas_call(kernel, out_shape=(jax.ShapeDtypeStruct((1, NX, FEATS, D),...]
    dot_general x4 -> x0, matrix products: 14.6 us -> none  [the longest x1 5.19 us: local(): jnp.einsum('tf,ktd->kfd', activation, used_grads, preferred_element_type=...]
    all_gather x1 -> x0, blocking collectives: 12.6 us -> none  [local(): local_grads = lax.all_gather(cotangent, 'layer', axis=0, tiled=True)]
  transfers between devices with their start and end apart: 3 -> 0, of which waited for: 3 -> 0; matrix products, arithmetic and copies ran while one was open for 1% -> 0% of each run, Pallas kernels for 0% -> 0%
where the time goes in v1:
time: 96.9 us; the launch traced here: 96.7 us
  Pallas kernels  89.1 us (92%)
  local copies, waits for them, and re-layouts  6.95 us (7%)
    pallas_call x1, Pallas kernels, local(): pl.pallas_call(kernel, out_shape=(jax.ShapeDtypeStruct((1, NX, FEATS, D),...  89.1 us
    unnamed x10, local copies, waits for them, and re-layouts  4.48 us
    pallas_call x1, local copies, waits for them, and re-layouts, local(): pl.pallas_call(kernel, out_shape=(jax.ShapeDtypeStruct((1, NX, FEATS, D),...  2.47 us

profile of v1, /device:TPU:1, one launch (start us, length us, event | category | flops | bytes accessed | tf_op | source)
XLA Modules:
  0.0 96.7 jit_solution(17827258810764397174)
XLA Ops:
  0.6 2.4 %copy.10.decw_hbm = bf16[1,4,256,576]{3,2,1,0:T(8,128)(2,1)} copy(bf16[1,4,256,576]{2,3,1,0:T(8,128)(2,1)} %param.10) | data formatting | bytes 2359296 | tf_op args[4]
  3.0 89.1 %shard_map.93 = (bf16[1,4,256,576]{3,2,1,0:T(8,128)(2,1)}, bf16[1,576,256]{2,1,0:T(8,128)(2,1)}, f32[1,256]{1,0:T(1,128)}, bf16[1,1024,256]{2,1,0:T(8,128)(2,1)}) custom-call(bf16[1,32,576]{2,1,0:T(8,128)(2,1)} %resid.1, bf16[1,32,576]{2,1,0:T(8,128)(2,1)} %cot.1, f32[1,256]{1,0:T(1,128)} %bias.1, bf16[1,576,256]{2,1,0:T(8,128)(2,1)} %encw_hbm.1, ...), custom_call_target="tpu_custom_call" | custom-call | tf_op jit(solution)/shard_map/pallas_call | solution.py:310
  92.1 0.0 copy-start.1
  92.1 0.0 copy-start.2
  92.2 0.0 copy-start
  92.2 2.5 %copy.11 = bf16[1,4,256,576]{2,3,1,0:T(8,128)(2,1)} copy(bf16[1,4,256,576]{3,2,1,0:T(8,128)(2,1)} %get-tuple-element.4) | data formatting | bytes 2359296 | tf_op jit(solution)/shard_map/pallas_call | solution.py:310
  94.6 0.0 copy-done.1
  94.6 0.7 copy.15
  95.3 0.0 copy-done.2
  95.4 0.6 copy.16
  95.9 0.0 copy-done
  95.9 0.8 copy.17
Async XLA Ops:
  92.1 2.5 %copy-start.1 = (bf16[1,576,256]{2,1,0:T(8,128)(2,1)S(1)}, bf16[1,576,256]{2,1,0:T(8,128)(2,1)}, u32[]{:S(2)}) copy-start(bf16[1,576,256]{2,1,0:T(8,128)(2,1)} %get-tuple-element.13) | copy-start | bytes 884740
  92.1 3.2 %copy-start.2 = (f32[1,256]{1,0:T(1,128)S(1)}, f32[1,256]{1,0:T(1,128)}, u32[]{:S(2)}) copy-start(f32[1,256]{1,0:T(1,128)} %get-tuple-element.14) | copy-start | bytes 3076
  92.2 3.8 %copy-start = (bf16[1,1024,256]{2,1,0:T(8,128)(2,1)S(1)}, bf16[1,1024,256]{2,1,0:T(8,128)(2,1)}, u32[]{:S(2)}) copy-start(bf16[1,1024,256]{2,1,0:T(8,128)(2,1)} %get-tuple-element.15) | copy-start | bytes 1572868

commit v2 on v0

v2 whole, which is shorter than its diff:
```python
import jax
import jax.numpy as jnp
from jax import lax
from jax.experimental import pallas as pl
from jax.experimental.pallas import tpu as pltpu
from jax.sharding import PartitionSpec as P

MESH = pl.DeviceIdType.MESH
BF16, F32 = jnp.bfloat16, jnp.float32

NX, NZ, NJ = 4, 8, 4
TOK = 32
ROWS = NJ * TOK
HALF = ROWS // 2
D = 576
PAD = 640
OFF = PAD - D
FEATS = 256
LAST = NZ - 1


def nn(a, b):
    return jnp.dot(a, b, preferred_element_type=F32)


def tn(a, b):
    return lax.dot_general(a, b, (((0,), (0,)), ((), ())), preferred_element_type=F32)


def kernel(
    resid, cot, bias, encw_hbm, decw_hbm, active_hbm,
    dec_out, enc_out, bias_out, fg_out,
    gp, cots, encw, ew, decw, dw, active,
    part, r1, s2, r2, af, acc, dec_st, enc_st,
    loc_sem, out_sem, p_recv, c_recv, zp_send, zt_send, yp_send, yt_send, xs_send, tx_send,
    r_recv, r_send,
):
    x = lax.axis_index("layer")
    f = lax.axis_index("feat")
    w = lax.axis_index("width")
    z, j = lax.div(f, NJ), lax.rem(f, NJ)
    c = lax.rem(w, 2)

    def at(dx=0, zz=None, jj=None, ww=None):
        zz = z if zz is None else zz
        jj = j if jj is None else jj
        return {"layer": lax.rem(x + dx, NX), "feat": zz * NJ + jj, "width": w if ww is None else ww}

    zi = lambda d: lax.rem(z + d + NZ, NZ)
    hop = (at(zz=zi(1)), at(zz=zi(-1)))
    core_peer = at(ww=w + 1 - 2 * c)
    far_peer = at(ww=lax.rem(w + 2, 4))
    order = [
        j,
        jnp.where(j == 0, 1, j - 1),
        jnp.where(j == 0, 2, jnp.where(j == 3, 1, j + 1)),
        jnp.where(j < 2, 3, 0),
    ]

    slot = lambda d: d + 3
    chunk = lambda d, i: slot(d) * NJ + order[i]

    def when(cond, fn):
        if cond is None:
            fn()
        else:
            pl.when(cond)(fn)

    loads = [
        (pltpu.make_async_copy(encw_hbm.at[0], encw, loc_sem.at[4]), None),
        (pltpu.make_async_copy(active_hbm.at[0], active, loc_sem.at[5]), None),
    ]
    for k in range(NX):
        loads.append((pltpu.make_async_copy(decw_hbm.at[0, jnp.minimum(x + k, NX - 1)], decw.at[k], loc_sem.at[k]), x + k < NX))

    barrier = pltpu.get_barrier_semaphore()
    peers = [core_peer, far_peer, hop[0], hop[1], at(1), at(2), at(3)] + [at(jj=order[i]) for i in (1, 2, 3)]
    for dev in peers:
        pl.semaphore_signal(barrier, inc=1, device_id=dev, device_id_type=MESH)
    gp[chunk(0, 0)] = jnp.concatenate([resid[0], cot[0]], axis=1)
    for cp, cond in loads:
        when(cond, cp.start)
    pl.semaphore_wait(barrier, len(peers))

    def remote(src, dst, ss, rs, dev):
        return pltpu.make_async_remote_copy(src, dst, ss, rs, device_id=dev, device_id_type=MESH)

    sent = []

    def send(cp, cond=None):
        sent.append((cp, cond))
        when(cond, cp.start)

    third = x <= 1
    relay = (x == 1) | (x == 2)

    def next_d(r, d):
        return 4 if r == 3 else (r + 1 if d else -r - 1)

    def here(r, d):
        return 4 if r == 4 else (r if d else -r)

    def send_z(r, i, d):
        a, b = chunk(here(r, d), i), chunk(next_d(r, d), i)
        send(remote(gp.at[a], gp.at[b], zp_send.at[d, a], p_recv.at[b], hop[d]))

    def send_zt(r, i, d):
        a, b = chunk(here(r, d), i), chunk(next_d(r, d), i)
        send(remote(cots.at[1, a], cots.at[1, b], zt_send.at[d, a], c_recv.at[1, b], hop[d]), third)

    def send_x(a):
        own = gp.at[a, :, pl.ds(2 * D - PAD, PAD)]
        send(remote(own, cots.at[0, a], xs_send.at[0, a], c_recv.at[0, a], at(3)), x >= 1)
        send(remote(own, cots.at[2, a], xs_send.at[1, a], c_recv.at[2, a], at(1)), x == 3)

    def wait_p(a):
        remote(gp.at[a], gp.at[a], zp_send.at[0, a], p_recv.at[a], hop[0]).wait_recv()

    def wait_c(k, a, cond):
        cp = remote(cots.at[k, a], cots.at[k, a], zp_send.at[0, a], c_recv.at[k, a], hop[0])
        when(cond, cp.wait_recv)

    def own():
        a = chunk(0, 0)
        for d in (0, 1):
            send_z(0, 0, d)
        for i in (1, 2, 3):
            send(remote(gp.at[a], gp.at[a], yp_send.at[i], p_recv.at[a], at(jj=order[i])))
        send(remote(gp.at[a, :, pl.ds(2 * D - PAD, PAD)], cots.at[1, a], tx_send.at[a], c_recv.at[1, a], at(2)), x >= 2)
        send_x(a)

    def t0():
        a = chunk(0, 0)
        wait_c(1, a, third)
        for i in (1, 2, 3):
            send(remote(cots.at[1, a], cots.at[1, a], yt_send.at[i], c_recv.at[1, a], at(jj=order[i])), third)

    def y(i):
        a = chunk(0, i)
        wait_p(a)
        for d in (0, 1):
            send_z(0, i, d)
        send_x(a)

    def ty(i):
        wait_c(1, chunk(0, i), third)
        for d in (0, 1):
            send_zt(0, i, d)

    def zp(r, i):
        for d in (0, 1):
            if r == 4 and (i < 2) != (d == 0):
                continue
            a = chunk(here(r, d), i)
            wait_p(a)
            if r < 3 or (r == 3 and (i < 2) == (d == 0)):
                send_z(r, i, d)
            send_x(a)

    def zt(r, i):
        for d in (0, 1):
            if r == 4 and (i == 1) != (d == 0):
                continue
            wait_c(1, chunk(here(r, d), i), third)
            if r < 3 or (r == 3 and (i == 1) == (d == 0)):
                send_zt(r, i, d)

    def rl(r):
        for d in (-r, r) if r < 4 else (4,):
            a = chunk(d, 0)
            wait_c(0, a, relay)
            send(remote(cots.at[0, a], cots.at[1, a], tx_send.at[a], c_recv.at[1, a], at(3)), relay)

    def setup():
        for cp, cond in loads:
            when(cond, cp.wait)
        ew[0:D, :] = encw[...]
        ew[D:PAD, :] = jnp.zeros((OFF, FEATS), BF16)
        for k in range(NX):
            @pl.when(x + k < NX)
            def _():
                dw[k, 0:OFF, :] = jnp.zeros((OFF, FEATS), BF16)
                dw[k, OFF:PAD, :] = decw[k]
        for t in range(NX):
            @pl.when(t < x)
            def _():
                dec_st[t] = jnp.zeros((D, FEATS), BF16)

    def compute(d):
        for i in range(NJ):
            a = chunk(d, i)
            wait_c(0, a, x == 0 if i == 0 and d != 0 else x <= 2)
            if i == 0 and d != 0:
                wait_c(1, a, third)
            wait_c(2, a, x == 0)
        s = slot(d)
        at_s = slice(s * NJ, (s + 1) * NJ)
        rows = gp[at_s]
        part[s, 0] = nn(rows[:, :, 0:PAD].reshape(ROWS, PAD), ew[...])
        part[s, 1] = nn(rows[:, :, 2 * D - PAD :].reshape(ROWS, PAD), dw[0])
        for k, cond in enumerate((x <= 2, x <= 1, x == 0)):
            @pl.when(cond)
            def _():
                part[s, 1] += nn(cots[k, at_s].reshape(ROWS, PAD), dw[k + 1])
        send(sum1(s))

    mine = pl.ds(pl.multiple_of(c * HALF, HALF), HALF)
    other = pl.ds(pl.multiple_of((1 - c) * HALF, HALF), HALF)
    sum1 = lambda s: remote(part.at[s, :, other], r1.at[s], r_send.at[0, s], r_recv.at[0, s], core_peer)
    sum2 = lambda s: remote(s2.at[s], r2.at[s], r_send.at[1, s], r_recv.at[1, s], far_peer)

    def sum3(s, half):
        rows = pl.ds(pl.multiple_of(s * ROWS + half * HALF, HALF), HALF)
        return remote(af.at[:, rows], af.at[:, rows], r_send.at[2, s], r_recv.at[2, s], core_peer)

    def red2(d):
        s = slot(d)
        sum1(s).wait_recv()
        s2[s] = (part[s, :, mine, :] + r1[s]).astype(BF16)
        send(sum2(s))

    def red3(d):
        s = slot(d)
        sum2(s).wait_recv()
        total = s2[s].astype(F32) + r2[s].astype(F32)
        gate = active[pl.ds(pl.multiple_of(zi(d) * ROWS + c * HALF, HALF), HALF), :].astype(F32)
        rows = pl.ds(pl.multiple_of(s * ROWS + c * HALF, HALF), HALF)
        af[0, rows, :] = ((total[0] + bias[...]) * gate).astype(BF16)
        af[1, rows, :] = (total[1] * gate).astype(BF16)
        send(sum3(s, c))

    def fg_copy(d):
        s = slot(d)
        return pltpu.make_async_copy(
            af.at[1, s * ROWS : (s + 1) * ROWS],
            fg_out.at[0, pl.ds(pl.multiple_of(zi(d) * ROWS, ROWS), ROWS)],
            out_sem.at[s],
        )

    def red4(d):
        sum3(slot(d), 1 - c).wait_recv()
        fg_copy(d).start()

    def dec_copy(t):
        return pltpu.make_async_copy(dec_st.at[t], dec_out.at[0, t], out_sem.at[NZ + t])

    enc_copy = pltpu.make_async_copy(enc_st, enc_out.at[0], out_sem.at[NZ + NX])

    def final(last):
        s = slice(LAST if last else 0, NZ if last else LAST)
        ch, rows = slice(s.start * NJ, s.stop * NJ), slice(s.start * ROWS, s.stop * ROWS)
        n = rows.stop - rows.start
        act, fg = af[0, rows], af[1, rows]

        def dec(k, data):
            g = tn(data.reshape(n, PAD), act)[OFF:]
            if last:
                t = x + k
                dec_st[t] = (acc[k] + g).astype(BF16)
                dec_copy(t).start()
            else:
                acc[k] = g

        g = tn(gp[ch, :, 0:PAD].reshape(n, PAD), fg)[0:D]
        b = jnp.sum(fg.astype(F32), axis=0, keepdims=True)
        if last:
            enc_st[...] = (acc[NX] + g).astype(BF16)
            enc_copy.start()
            bias_out[...] += b
        else:
            acc[NX] = g
            bias_out[...] = b
        dec(0, gp[ch, :, 2 * D - PAD :])
        for k in range(1, NX):
            pl.when(x + k < NX)(lambda: dec(k, cots[k - 1, ch]))


    own()
    y(1), zp(1, 0), t0(), y(2), zp(1, 1), y(3)
    setup()
    for t in range(NX):
        pl.when(t < x)(lambda: dec_copy(t).start())
    ty(1), zp(1, 2), ty(2), zp(1, 3), ty(3), rl(1)
    zt(1, 1), zp(2, 0), compute(0), zt(1, 2), zp(2, 1), zt(1, 3), zp(2, 2), rl(2)
    red2(0), compute(-1), zt(2, 1), zp(2, 3), compute(1), zt(2, 2), zp(3, 0)
    red2(-1), red3(0), zt(2, 3), zp(3, 1), red2(1), compute(-2), rl(3), zt(3, 1), zp(3, 2)
    compute(2), red3(-1), zt(3, 2), zp(3, 3), red2(-2), red3(1), zp(4, 0), zp(4, 2), zt(3, 3)
    red2(2), compute(-3), rl(4), zp(4, 1), zp(4, 3), red3(-2), compute(3), red3(2)
    zt(4, 1), zt(4, 2), zt(4, 3)
    red2(-3), red2(3), compute(4), red3(-3), red3(3), red2(4)
    for d in range(-3, 4):
        red4(d)
    final(False)
    red3(4), red4(4)
    final(True)
    for cp, cond in sent:
        when(cond, cp.wait_send)
    for d in range(-3, 5):
        fg_copy(d).wait()
    for t in range(NX):
        dec_copy(t).wait()
    enc_copy.wait()


def local(residuals, cotangent, enc_weight, enc_bias, dec_weight, active):
    vmem, hbm = pl.BlockSpec(memory_space=pltpu.VMEM), pl.BlockSpec(memory_space=pl.ANY)
    chunks, dma = NZ * NJ, pltpu.SemaphoreType.DMA
    dec_grad, enc_grad, bias_grad, feat_grad = pl.pallas_call(
        kernel,
        out_shape=(
            jax.ShapeDtypeStruct((1, NX, D, FEATS), BF16),
            jax.ShapeDtypeStruct((1, D, FEATS), BF16),
            jax.ShapeDtypeStruct((1, FEATS), F32),
            jax.ShapeDtypeStruct((1, NZ * ROWS, FEATS), BF16),
        ),
        in_specs=[vmem, vmem, vmem, hbm, hbm, hbm],
        out_specs=(hbm, hbm, vmem, hbm),
        scratch_shapes=[
            pltpu.VMEM((chunks, TOK, 2 * D), BF16),
            pltpu.VMEM((3, chunks, TOK, PAD), BF16),
            pltpu.VMEM((D, FEATS), BF16),
            pltpu.VMEM((PAD, FEATS), BF16),
            pltpu.VMEM((NX, D, FEATS), BF16),
            pltpu.VMEM((NX, PAD, FEATS), BF16),
            pltpu.VMEM((NZ * ROWS, FEATS), jnp.int32),
            pltpu.VMEM((NZ, 2, ROWS, FEATS), F32),
            pltpu.VMEM((NZ, 2, HALF, FEATS), F32),
            pltpu.VMEM((NZ, 2, HALF, FEATS), BF16),
            pltpu.VMEM((NZ, 2, HALF, FEATS), BF16),
            pltpu.VMEM((2, NZ * ROWS, FEATS), BF16),
            pltpu.VMEM((NX + 1, D, FEATS), F32),
            pltpu.VMEM((NX, D, FEATS), BF16),
            pltpu.VMEM((D, FEATS), BF16),
            dma((6,)),
            dma((NZ + NX + 1,)),
            dma((chunks,)),
            dma((3, chunks)),
            dma((2, chunks)),
            dma((2, chunks)),
            dma((NJ,)),
            dma((NJ,)),
            dma((2, chunks)),
            dma((chunks,)),
            dma((3, NZ)),
            dma((3, NZ)),
        ],
        compiler_params=pltpu.CompilerParams(collective_id=0, has_side_effects=True, vmem_limit_bytes=60 * 2**20),
    )(residuals, cotangent, enc_bias, enc_weight, jnp.swapaxes(dec_weight, 2, 3), active)
    return jnp.swapaxes(dec_grad, 2, 3), enc_grad, bias_grad, feat_grad


def solution(mesh):
    in_specs = (
        P("layer", "feat", "width"),
        P("layer", "feat", "width"),
        P("layer", "width", "feat"),
        P("layer", "feat"),
        P("layer", None, "feat", "width"),
        P("layer", None, "feat"),
    )
    out_specs = (
        P("layer", None, "feat", "width"),
        P("layer", "width", "feat"),
        P("layer", "feat"),
        P("layer", None, "feat"),
    )
    return jax.shard_map(local, mesh=mesh, in_specs=in_specs, out_specs=out_specs, check_vma=False)
```

time: 467 us -> 87 us (0.19)
  waiting for transfers between devices: 424 us -> 0 us
  Pallas kernels: 0 us -> 81.6 us
  matrix products: 14.6 us -> 0 us
  between operations: 13.8 us -> 0.67 us
  blocking collectives: 12.6 us -> 0 us
    all_gather x2 -> x0, waiting for transfers between devices: 299 us -> none  [the longest x1 171 us: local(): lax.all_gather(local_grads, 'feat', axis=1, tiled=True)]
    psum x1 -> x0, waiting for transfers between devices: 124 us -> none  [local(): enc_total, feat_total = lax.psum((enc_part, feat_part), 'width')]
    pallas_call x0 -> x1, Pallas kernels: none -> 81.6 us  [local(): pl.pallas_call(kernel, out_shape=(jax.ShapeDtypeStruct((1, NX, D, FEATS),...]
    dot_general x4 -> x0, matrix products: 14.6 us -> none  [the longest x1 5.19 us: local(): jnp.einsum('tf,ktd->kfd', activation, used_grads, preferred_element_type=...]
    all_gather x1 -> x0, blocking collectives: 12.6 us -> none  [local(): local_grads = lax.all_gather(cotangent, 'layer', axis=0, tiled=True)]
  transfers between devices with their start and end apart: 3 -> 0, of which waited for: 3 -> 0; matrix products, arithmetic and copies ran while one was open for 1% -> 0% of each run, Pallas kernels for 0% -> 0%
where the time goes in v2:
time: 87 us; the launch traced here: 86.8 us
  Pallas kernels  81.6 us (94%)
  local copies, waits for them, and re-layouts  4.51 us (5%)
    pallas_call x1, Pallas kernels, local(): pl.pallas_call(kernel, out_shape=(jax.ShapeDtypeStruct((1, NX, D, FEATS),...  81.6 us
    unnamed x10, local copies, waits for them, and re-layouts  4.51 us

profile of v2, /device:TPU:1, one launch (start us, length us, event | category | flops | bytes accessed | tf_op | source)
XLA Modules:
  0.0 86.8 jit_solution(4429608993818516117)
XLA Ops:
  0.6 81.6 %shard_map.93 = (bf16[1,4,576,256]{3,2,1,0:T(8,128)(2,1)}, bf16[1,576,256]{2,1,0:T(8,128)(2,1)}, f32[1,256]{1,0:T(1,128)}, bf16[1,1024,256]{2,1,0:T(8,128)(2,1)}) custom-call(bf16[1,32,576]{2,1,0:T(8,128)(2,1)} %resid.1, bf16[1,32,576]{2,1,0:T(8,128)(2,1)} %cot.1, f32[1,256]{1,0:T(1,128)} %bias.1, bf16[1,576,256]{2,1,0:T(8,128)(2,1)} %encw_hbm.1, ...), custom_call_target="tpu_custom_call" | custom-call | tf_op jit(solution)/shard_map/pallas_call | solution.py:308
  82.3 0.0 copy-start.1
  82.3 0.0 copy-start.2
  82.3 0.0 copy-start
  82.3 2.4 %copy.14 = bf16[1,4,256,576]{2,3,1,0:T(8,128)(2,1)} copy(bf16[1,4,256,576]{2,3,1,0:T(8,128)(2,1)} %bitcast.3) | data formatting | bytes 2359296
  84.7 0.0 copy-done.1
  84.7 0.7 copy.15
  85.4 0.0 copy-done.2
  85.4 0.6 copy.16
  86.0 0.0 copy-done
  86.0 0.8 copy.17
Async XLA Ops:
  82.3 2.5 %copy-start.1 = (bf16[1,576,256]{2,1,0:T(8,128)(2,1)S(1)}, bf16[1,576,256]{2,1,0:T(8,128)(2,1)}, u32[]{:S(2)}) copy-start(bf16[1,576,256]{2,1,0:T(8,128)(2,1)} %get-tuple-element.17) | copy-start | bytes 884740
  82.3 3.2 %copy-start.2 = (f32[1,256]{1,0:T(1,128)S(1)}, f32[1,256]{1,0:T(1,128)}, u32[]{:S(2)}) copy-start(f32[1,256]{1,0:T(1,128)} %get-tuple-element.18) | copy-start | bytes 3076
  82.3 3.7 %copy-start = (bf16[1,1024,256]{2,1,0:T(8,128)(2,1)S(1)}, bf16[1,1024,256]{2,1,0:T(8,128)(2,1)}, u32[]{:S(2)}) copy-start(bf16[1,1024,256]{2,1,0:T(8,128)(2,1)} %get-tuple-element.19) | copy-start | bytes 1572868

commit v3 on v2

v3 whole, which is shorter than its diff:
```python
import jax
import jax.numpy as jnp
from jax import lax
from jax.experimental import pallas as pl
from jax.experimental.pallas import tpu as pltpu
from jax.sharding import PartitionSpec as P

MESH = pl.DeviceIdType.MESH
BF16, F32 = jnp.bfloat16, jnp.float32

NX, NZ, NJ = 4, 8, 4
TOK = 32
SUB = TOK // 2
HALF = NJ * SUB
D = 576
MAIN = 512
TAIL = D - MAIN
WIDE = 2 * D
FEATS = 256
CHUNKS = NZ * NJ
LAST = NZ - 1


def nn(a, b):
    return jnp.dot(a, b, preferred_element_type=F32)


def tn(a, b):
    return lax.dot_general(a, b, (((0,), (0,)), ((), ())), preferred_element_type=F32)


def gather_kernel(
    resid_hbm, cot_hbm, bias_hbm, encw_hbm, decw_hbm, active_hbm,
    dec_out, enc_out, bias_out, fg_out,
    raw, gp, cots, weight, wtail, bias, active,
    part, r1, s2, r2, af, acc, bias_acc,
    loc_sem, p_recv, c_recv, zp_send, zt_send, yp_send, yt_send, xs_send, tx_send,
    r_recv, r_send,
):
    x = lax.axis_index("layer")
    f = lax.axis_index("feat")
    w = lax.axis_index("width")
    z, j = lax.div(f, NJ), lax.rem(f, NJ)
    c = lax.rem(w, 2)

    def at(dx=0, zz=None, jj=None, ww=None):
        zz = z if zz is None else zz
        jj = j if jj is None else jj
        return {"layer": lax.rem(x + dx, NX), "feat": zz * NJ + jj, "width": w if ww is None else ww}

    zi = lambda d: lax.rem(z + d + NZ, NZ)
    hop = (at(zz=zi(1)), at(zz=zi(-1)))
    core_peer = at(ww=w + 1 - 2 * c)
    far_peer = at(ww=lax.rem(w + 2, 4))
    order = [
        j,
        jnp.where(j == 0, 1, j - 1),
        jnp.where(j == 0, 2, jnp.where(j == 3, 1, j + 1)),
        jnp.where(j < 2, 3, 0),
    ]

    slot = lambda d: d + 3
    chunk = lambda d, i: slot(d) * NJ + order[i]

    def when(cond, fn):
        if cond is None:
            fn()
        else:
            pl.when(cond)(fn)

    barrier = pltpu.get_barrier_semaphore()
    peers = [core_peer, far_peer, hop[0], hop[1], at(1), at(2), at(3)] + [at(jj=order[i]) for i in (1, 2, 3)]
    for dev in peers:
        pl.semaphore_signal(barrier, inc=1, device_id=dev, device_id_type=MESH)

    first = [
        pltpu.make_async_copy(resid_hbm.at[0], raw.at[0], loc_sem.at[0]),
        pltpu.make_async_copy(cot_hbm.at[0], raw.at[1], loc_sem.at[1]),
    ]
    for cp in first:
        cp.start()
    loads = [
        (pltpu.make_async_copy(encw_hbm.at[0], weight.at[0], loc_sem.at[2]), None),
        (pltpu.make_async_copy(active_hbm.at[:, c], active, loc_sem.at[3]), None),
        (pltpu.make_async_copy(bias_hbm, bias, loc_sem.at[4]), None),
    ]
    for k in range(NX):
        cp = pltpu.make_async_copy(decw_hbm.at[0, jnp.minimum(x + k, NX - 1)], weight.at[k + 1], loc_sem.at[5 + k])
        loads.append((cp, x + k < NX))
    for cp, cond in loads:
        when(cond, cp.start)

    mine = chunk(0, 0)
    for u in (0, 1):
        first[u].wait()
        rows = raw[u]
        gp[mine, u, :, 0:MAIN] = rows[0:SUB, 0:MAIN]
        gp[mine, u, :, MAIN : 2 * MAIN] = rows[SUB:TOK, 0:MAIN]
        gp[mine, u, :, 2 * MAIN : WIDE] = jnp.concatenate([rows[0:SUB, MAIN:D], rows[SUB:TOK, MAIN:D]], axis=1)
    pl.semaphore_wait(barrier, len(peers))

    def remote(src, dst, ss, rs, dev):
        return pltpu.make_async_remote_copy(src, dst, ss, rs, device_id=dev, device_id_type=MESH)

    sent = []

    def send(cp, cond=None):
        sent.append((cp, cond))
        when(cond, cp.start)

    third = x <= 1

    def next_d(r, d):
        return 4 if r == 3 else (r + 1 if d else -r - 1)

    def here(r, d):
        return 4 if r == 4 else (r if d else -r)

    def send_z(r, i, d):
        a, b = chunk(here(r, d), i), chunk(next_d(r, d), i)
        send(remote(gp.at[a], gp.at[b], zp_send.at[d, a], p_recv.at[b], hop[d]))

    def send_zt(r, i, d):
        a, b = chunk(here(r, d), i), chunk(next_d(r, d), i)
        send(remote(cots.at[1, a], cots.at[1, b], zt_send.at[d, a], c_recv.at[1, b], hop[d]), third)

    def send_x(a, i):
        own = gp.at[a, 1]
        send(remote(own, cots.at[0, a], xs_send.at[0, a], c_recv.at[0, a], at(3)), x >= 1)
        send(remote(own, cots.at[2, a], xs_send.at[1, a], c_recv.at[2, a], at(1)), x == 3)
        if i == 1:
            send(remote(own, cots.at[1, a], xs_send.at[1, a], c_recv.at[1, a], at(1)), x == 2)

    def wait_p(a):
        remote(gp.at[a], gp.at[a], zp_send.at[0, a], p_recv.at[a], hop[0]).wait_recv()

    def wait_c(k, a, cond):
        cp = remote(cots.at[k, a], cots.at[k, a], zp_send.at[0, a], c_recv.at[k, a], hop[0])
        when(cond, cp.wait_recv)

    def own():
        for d in (0, 1):
            send_z(0, 0, d)
        send(remote(gp.at[mine, 1], cots.at[1, mine], tx_send.at[mine], c_recv.at[1, mine], at(2)), x >= 2)
        for i in (1, 2, 3):
            send(remote(gp.at[mine], gp.at[mine], yp_send.at[i], p_recv.at[mine], at(jj=order[i])))
        send_x(mine, 0)

    def t0():
        wait_c(1, mine, third)
        for i, cond in ((1, j >= 2), (2, (j == 0) | (j == 3)), (3, None)):
            cp = remote(cots.at[1, mine], cots.at[1, mine], yt_send.at[i], c_recv.at[1, mine], at(jj=order[i]))
            send(cp, third if cond is None else third & cond)

    def y(i):
        a = chunk(0, i)
        wait_p(a)
        for d in (0, 1):
            send_z(0, i, d)
        send_x(a, i)

    def ty(i):
        wait_c(1, chunk(0, i), third)
        for d in (0, 1):
            send_zt(0, i, d)

    def zp(r, i):
        for d in (0, 1):
            if r == 4 and (i < 2) != (d == 0):
                continue
            a = chunk(here(r, d), i)
            wait_p(a)
            if r < 3 or (r == 3 and (i < 2) == (d == 0)):
                send_z(r, i, d)
            send_x(a, i)

    def zt(r, i):
        for d in (0, 1):
            if r == 4 and (i == 2) != (d == 0):
                continue
            wait_c(1, chunk(here(r, d), i), third)
            if r < 3 or (r == 3 and (i == 2) == (d == 0)):
                send_zt(r, i, d)

    def rl(r):
        def hand(k, a, cond, dx):
            wait_c(k, a, cond)
            send(remote(cots.at[k, a], cots.at[1, a], tx_send.at[a], c_recv.at[1, a], at(dx)), cond)

        for d in (0,) if r == 0 else (4,) if r == 4 else (-r, r):
            if d:
                hand(0, chunk(d, 0), x == 1, 3)
                hand(2, chunk(d, 0), x == 0, 1)
            hand(1, chunk(d, 1), x == 3, 1)
            hand(2, chunk(d, 1), x == 0, 1)

    def setup():
        for cp, cond in loads:
            when(cond, cp.wait)
        wtail[...] = jnp.zeros_like(wtail)
        for k in range(NX + 1):
            wtail[k, 0:TAIL, 0:FEATS] = weight[k, MAIN:D, :]
            wtail[k, TAIL : 2 * TAIL, FEATS : 2 * FEATS] = weight[k, MAIN:D, :]
        for t in range(NX):
            @pl.when(t < x)
            def _():
                dec_out[t] = jnp.zeros((D, FEATS), BF16)

    def compute(d):
        for i in range(NJ):
            a = chunk(d, i)
            wait_c(0, a, (x == 0) | (x == 2) if i == 0 and d else x <= 2)
            if i == 1 or (i == 0 and d):
                wait_c(1, a, third)
            if i > 1 or (i == 0 and d == 0):
                wait_c(2, a, x == 0)
        s = slot(d)
        ch = slice(s * NJ, (s + 1) * NJ)

        def times(data, k):
            both = jnp.concatenate(
                [data[:, :, 0:MAIN].reshape(HALF, MAIN), data[:, :, MAIN : 2 * MAIN].reshape(HALF, MAIN)], axis=0
            )
            main = nn(both, weight[k, 0:MAIN, :])
            tails = nn(data[:, :, 2 * MAIN :].reshape(HALF, 2 * TAIL), wtail[k])
            return main[0:HALF] + tails[:, 0:FEATS], main[HALF:] + tails[:, FEATS:]

        for k in (0, 1):
            part[s, 0, k], part[s, 1, k] = times(gp[ch, k], k)
        for k, cond in enumerate((x <= 2, x <= 1, x == 0)):
            @pl.when(cond)
            def _():
                a, b = times(cots[k, ch], k + 2)
                part[s, 0, 1] += a
                part[s, 1, 1] += b
        send(sum1(s))

    sum1 = lambda s: remote(part.at[s, 1 - c], r1.at[s], r_send.at[0, s], r_recv.at[0, s], core_peer)
    sum2 = lambda s: remote(s2.at[s], r2.at[s], r_send.at[1, s], r_recv.at[1, s], far_peer)

    def sum3(s, half):
        block = af.at[half, :, s * HALF : (s + 1) * HALF]
        return remote(block, block, r_send.at[2, s], r_recv.at[2, s], core_peer)

    def red2(d):
        s = slot(d)
        sum1(s).wait_recv()
        s2[s] = (part[s, c] + r1[s]).astype(BF16)
        send(sum2(s))

    def red3(d):
        s = slot(d)
        sum2(s).wait_recv()
        total = s2[s].astype(F32) + r2[s].astype(F32)
        gate = active[pl.ds(zi(d) * NJ, NJ)].reshape(HALF, FEATS).astype(F32)
        rows = slice(s * HALF, (s + 1) * HALF)
        af[c, 0, rows, :] = ((total[0] + bias[...]) * gate).astype(BF16)
        af[c, 1, rows, :] = (total[1] * gate).astype(BF16)
        send(sum3(s, c))

    def red4(d):
        s = slot(d)
        sum3(s, 1 - c).wait_recv()
        for h in (0, 1):
            fg_out[pl.ds(zi(d) * NJ, NJ), h] = af[h, 1, s * HALF : (s + 1) * HALF].reshape(NJ, SUB, FEATS)

    def final(last):
        lo, hi = (LAST, NZ) if last else (0, LAST)
        ch, rows = slice(lo * NJ, hi * NJ), slice(lo * HALF, hi * HALF)
        n = (hi - lo) * HALF

        def grads(data, k):
            a, b = af[0, k, rows], af[1, k, rows]
            main = tn(data[:, :, 0:MAIN].reshape(n, MAIN), a) + tn(data[:, :, MAIN : 2 * MAIN].reshape(n, MAIN), b)
            tails = data[:, :, 2 * MAIN :].reshape(n, 2 * TAIL)
            return main, tn(tails, a)[0:TAIL] + tn(tails, b)[TAIL:]

        def put(k, g, write):
            for piece, at_rows in zip(g, (slice(0, MAIN), slice(MAIN, D))):
                if last:
                    write(at_rows, (acc[k, at_rows] + piece).astype(BF16))
                else:
                    acc[k, at_rows] = piece

        def dec(k, data):
            def write(at_rows, v):
                dec_out[x + k, at_rows] = v

            put(k, grads(data, 0), write)

        def write_enc(at_rows, v):
            enc_out[at_rows] = v

        put(NX, grads(gp[ch, 0], 1), write_enc)
        sums = sum(jnp.sum(af[h, 1, rows].astype(F32), axis=0, keepdims=True) for h in (0, 1))
        if last:
            bias_out[...] = bias_acc[...] + sums
        else:
            bias_acc[...] = sums
        dec(0, gp[ch, 1])
        for k in range(1, NX):
            pl.when(x + k < NX)(lambda: dec(k, cots[k - 1, ch]))

    own()
    y(1), zp(1, 0), y(2), zp(1, 1), y(3), t0()
    setup()
    zp(1, 2), ty(2), rl(0), zp(1, 3), ty(3), zp(2, 0), rl(1), zp(2, 1), compute(0)
    zt(1, 2), zp(2, 2), zt(1, 3), compute(-1), zp(2, 3), red2(0), compute(1), rl(2)
    zp(3, 0), zt(2, 2), zp(3, 1), red2(-1), zt(2, 3), red2(1), compute(-2), zp(3, 2), compute(2)
    zp(3, 3), rl(3), zt(3, 2), red2(-2), zt(3, 3), zp(4, 0), zp(4, 2), red2(2), compute(-3)
    zp(4, 1), zp(4, 3), compute(3), rl(4), red2(-3), zt(4, 2), zt(4, 3), red2(3)
    compute(4), red3(0), red3(-1), red2(4)
    for d in (1, -2, 2, -3, 3):
        red3(d)
    for d in range(-3, 4):
        red4(d)
    final(False)
    red3(4), red4(4)
    final(True)
    for cp, cond in sent:
        when(cond, cp.wait_send)


def write_kernel(dec, enc, bias, fg, dec_out, enc_out, bias_out, fg_out, sem):
    copies = [
        pltpu.make_async_copy(dec, dec_out, sem.at[0]),
        pltpu.make_async_copy(enc, enc_out, sem.at[1]),
        pltpu.make_async_copy(bias, bias_out, sem.at[2]),
        pltpu.make_async_copy(fg, fg_out, sem.at[3]),
    ]
    for cp in copies:
        cp.start()
    for cp in copies:
        cp.wait()


def local(residuals, cotangent, enc_weight, enc_bias, dec_weight, active):
    vmem, hbm = pl.BlockSpec(memory_space=pltpu.VMEM), pl.BlockSpec(memory_space=pltpu.HBM)
    dma = pltpu.SemaphoreType.DMA
    outs = [((NX, D, FEATS), BF16), ((D, FEATS), BF16), ((1, FEATS), F32), ((CHUNKS, 2, SUB, FEATS), BF16)]
    held = pl.pallas_call(
        gather_kernel,
        out_shape=tuple(pltpu.VMEM(shape, dtype) for shape, dtype in outs),
        in_specs=[hbm] * 6,
        out_specs=(vmem,) * 4,
        scratch_shapes=[
            pltpu.VMEM((2, TOK, D), BF16),
            pltpu.VMEM((CHUNKS, 2, SUB, WIDE), BF16),
            pltpu.VMEM((3, CHUNKS, SUB, WIDE), BF16),
            pltpu.VMEM((NX + 1, D, FEATS), BF16),
            pltpu.VMEM((NX + 1, 2 * TAIL, 2 * FEATS), BF16),
            pltpu.VMEM((1, FEATS), F32),
            pltpu.VMEM((CHUNKS, SUB, FEATS), jnp.int32),
            pltpu.VMEM((NZ, 2, 2, HALF, FEATS), F32),
            pltpu.VMEM((NZ, 2, HALF, FEATS), F32),
            pltpu.VMEM((NZ, 2, HALF, FEATS), BF16),
            pltpu.VMEM((NZ, 2, HALF, FEATS), BF16),
            pltpu.VMEM((2, 2, NZ * HALF, FEATS), BF16),
            pltpu.VMEM((NX + 1, D, FEATS), F32),
            pltpu.VMEM((1, FEATS), F32),
            dma((5 + NX,)),
            dma((CHUNKS,)),
            dma((3, CHUNKS)),
            dma((2, CHUNKS)),
            dma((2, CHUNKS)),
            dma((NJ,)),
            dma((NJ,)),
            dma((2, CHUNKS)),
            dma((CHUNKS,)),
            dma((3, NZ)),
            dma((3, NZ)),
        ],
        compiler_params=pltpu.CompilerParams(collective_id=0, has_side_effects=True, vmem_limit_bytes=62 * 2**20),
    )(
        residuals,
        cotangent,
        enc_bias,
        enc_weight,
        jnp.swapaxes(dec_weight, 2, 3),
        active.reshape(CHUNKS, 2, SUB, FEATS),
    )
    dec_grad, enc_grad, bias_grad, feat_grad = pl.pallas_call(
        write_kernel,
        out_shape=tuple(jax.ShapeDtypeStruct(shape, dtype) for shape, dtype in outs),
        in_specs=[vmem] * 4,
        out_specs=(hbm,) * 4,
        scratch_shapes=[dma((4,))],
        compiler_params=pltpu.CompilerParams(vmem_limit_bytes=8 * 2**20),
    )(*held)
    return (
        jnp.swapaxes(dec_grad, 1, 2)[None],
        enc_grad[None],
        bias_grad,
        feat_grad.reshape(1, CHUNKS * TOK, FEATS),
    )


def solution(mesh):
    in_specs = (
        P("layer", "feat", "width"),
        P("layer", "feat", "width"),
        P("layer", "width", "feat"),
        P("layer", "feat"),
        P("layer", None, "feat", "width"),
        P("layer", None, "feat"),
    )
    out_specs = (
        P("layer", None, "feat", "width"),
        P("layer", "width", "feat"),
        P("layer", "feat"),
        P("layer", None, "feat"),
    )
    return jax.shard_map(local, mesh=mesh, in_specs=in_specs, out_specs=out_specs, check_vma=False)
```

time: 87 us -> 73.9 us (0.85)
  Pallas kernels: 81.6 us -> 72.9 us
  local copies, waits for them, and re-layouts: 4.51 us -> 0 us
    pallas_call x1 -> x2, Pallas kernels: 81.6 us -> 72.9 us  [the longest x1 71.6 us: local(): pl.pallas_call(gather_kernel, out_shape=tuple((pltpu.VMEM(shape, dtype) f...]
    unnamed x10 -> x0, local copies, waits for them, and re-layouts: 4.51 us -> none
where the time goes in v3:
time: 73.9 us; the launch traced here: 73.5 us
  Pallas kernels  72.9 us (99%)
    pallas_call x1, Pallas kernels, local(): pl.pallas_call(gather_kernel, out_shape=tuple((pltpu.VMEM(shape, dtype) f...  71.6 us

profile of v3, /device:TPU:1, one launch (start us, length us, event | category | flops | bytes accessed | tf_op | source)
XLA Modules:
  0.0 73.5 jit_solution(16485611278082815522)
XLA Ops:
  0.6 71.6 %shard_map.93 = (bf16[4,576,256]{2,1,0:T(8,128)(2,1)S(1)}, bf16[576,256]{1,0:T(8,128)(2,1)S(1)}, f32[1,256]{1,0:T(1,128)S(1)}, bf16[32,2,16,256]{3,2,1,0:T(8,128)(2,1)S(1)}) custom-call(bf16[1,32,576]{2,1,0:T(8,128)(2,1)} %resid_hbm.1, bf16[1,32,576]{2,1,0:T(8,128)(2,1)} %cot_hbm.1, f32[1,256]{1,0:T(1,128)} %bias_hbm.1, bf16[1,576,256]{2,1,0:T(8,128)(2,1)} %encw_hbm.1, ...), custom_call_target="tpu_custom_call" | custom-call | tf_op jit(solution)/shard_map/pallas_call | solution.py:341
  72.2 1.3 %shard_map.94 = (bf16[4,576,256]{2,1,0:T(8,128)(2,1)}, bf16[576,256]{1,0:T(8,128)(2,1)}, f32[1,256]{1,0:T(1,128)}, bf16[32,2,16,256]{3,2,1,0:T(8,128)(2,1)}) custom-call(bf16[4,576,256]{2,1,0:T(8,128)(2,1)S(1)} %get-tuple-element.12.dec, bf16[576,256]{1,0:T(8,128)(2,1)S(1)} %get-tuple-element.13.enc, f32[1,256]{1,0:T(1,128)S(1)} %get-tuple-element.14.bias, ...), custom_call_target="tpu_custom_call" | custom-call | tf_op jit(solution)/shard_map/pallas_call | solution.py:382

commit v4 on v3

v4 whole, which is shorter than its diff:
```python
import jax
import jax.numpy as jnp
from jax import lax
from jax.experimental import pallas as pl
from jax.experimental.pallas import tpu as pltpu
from jax.sharding import PartitionSpec as P

MESH = pl.DeviceIdType.MESH
BF16, F32 = jnp.bfloat16, jnp.float32

NX, NZ, NJ = 4, 8, 4
TOK = 32
SUB = TOK // 2
HALF = NJ * SUB
D = 576
MAIN = 512
TAIL = D - MAIN
WIDE = 2 * D
FEATS = 256
CHUNKS = NZ * NJ
RING = (1, 2, 3)


def nn(a, b):
    return jnp.dot(a, b, preferred_element_type=F32)


def tn(a, b):
    return lax.dot_general(a, b, (((0,), (0,)), ((), ())), preferred_element_type=F32)


def gather_kernel(
    resid_hbm, cot_hbm, bias_hbm, encw_hbm, decw_hbm, active_hbm,
    dec_out, enc_out, bias_out, fg_out,
    raw, gp, cots, weight, wtail, bias, active,
    part, r1, s2, r2, af,
    loc_sem, p_recv, c_recv, t_recv, z_send, zt_send, y_send, yt_send, x_send,
    r_recv, r_send,
):
    x = lax.axis_index("layer")
    f = lax.axis_index("feat")
    w = lax.axis_index("width")
    z, j = lax.div(f, NJ), lax.rem(f, NJ)
    c = lax.rem(w, 2)

    def at(dx=0, zz=None, jj=None, ww=None):
        zz = z if zz is None else zz
        jj = j if jj is None else jj
        return {"layer": lax.rem(x + dx, NX), "feat": zz * NJ + jj, "width": w if ww is None else ww}

    zi = lambda d: lax.rem(z + d + NZ, NZ)
    hop = (at(zz=zi(1)), at(zz=zi(-1)))
    core_peer = at(ww=w + 1 - 2 * c)
    far_peer = at(ww=lax.rem(w + 2, 4))
    order = [
        j,
        jnp.where(j == 0, 1, j - 1),
        jnp.where(j == 0, 2, jnp.where(j == 3, 1, j + 1)),
        jnp.where(j < 2, 3, 0),
    ]

    slot = lambda d: d + 3
    chunk = lambda d, i: slot(d) * NJ + order[i]

    def when(cond, fn):
        if cond is None:
            fn()
        else:
            pl.when(cond)(fn)

    barrier = pltpu.get_barrier_semaphore()
    peers = [core_peer, far_peer, hop[0], hop[1], at(1), at(2), at(3)] + [at(jj=order[i]) for i in (1, 2, 3)]
    for dev in peers:
        pl.semaphore_signal(barrier, inc=1, device_id=dev, device_id_type=MESH)

    first = [
        pltpu.make_async_copy(resid_hbm.at[0], raw.at[0], loc_sem.at[0]),
        pltpu.make_async_copy(cot_hbm.at[0], raw.at[1], loc_sem.at[1]),
    ]
    for cp in first:
        cp.start()
    loads = [
        (pltpu.make_async_copy(encw_hbm.at[0], weight.at[0], loc_sem.at[2]), None),
        (pltpu.make_async_copy(active_hbm.at[:, c], active, loc_sem.at[3]), None),
        (pltpu.make_async_copy(bias_hbm, bias, loc_sem.at[4]), None),
    ]
    for k in range(NX):
        cp = pltpu.make_async_copy(decw_hbm.at[0, jnp.minimum(x + k, NX - 1)], weight.at[k + 1], loc_sem.at[5 + k])
        loads.append((cp, x + k < NX))
    for cp, cond in loads:
        when(cond, cp.start)

    mine = chunk(0, 0)
    for u in (0, 1):
        first[u].wait()
        rows = raw[u]
        gp[mine, u, :, 0:MAIN] = rows[0:SUB, 0:MAIN]
        gp[mine, u, :, MAIN : 2 * MAIN] = rows[SUB:TOK, 0:MAIN]
        gp[mine, u, :, 2 * MAIN : WIDE] = jnp.concatenate([rows[0:SUB, MAIN:D], rows[SUB:TOK, MAIN:D]], axis=1)
    pl.semaphore_wait(barrier, len(peers))

    def remote(src, dst, ss, rs, dev):
        return pltpu.make_async_remote_copy(src, dst, ss, rs, device_id=dev, device_id_type=MESH)

    def send(cp, cond=None):
        when(cond, cp.start)

    third = x <= 1

    def next_d(r, d):
        return 4 if r == 3 else (r + 1 if d else -r - 1)

    def here(r, d):
        return 4 if r == 4 else (r if d else -r)

    def send_z(r, i, d):
        a, b = chunk(here(r, d), i), chunk(next_d(r, d), i)
        send(remote(gp.at[a], gp.at[b], z_send.at[d], p_recv.at[b], hop[d]))

    def send_zt(r, i, d):
        a, b = chunk(here(r, d), i), chunk(next_d(r, d), i)
        send(remote(cots.at[1, a], cots.at[1, b], zt_send.at[d], t_recv.at[b], hop[d]), third)

    def send_x(a, d, i):
        own, s = gp.at[a, 1], slot(d)
        send(remote(own, cots.at[0, a], x_send.at[0], c_recv.at[0, s], at(3)), x >= 1)
        send(remote(own, cots.at[2, a], x_send.at[1], c_recv.at[1, s], at(1)), x == 3)
        if i not in RING or (d == 0 and i == 0):
            send(remote(own, cots.at[1, a], x_send.at[2], t_recv.at[a], at(2)), x >= 2)

    def wait_p(a):
        remote(gp.at[a], gp.at[a], z_send.at[0], p_recv.at[a], hop[0]).wait_recv()

    def wait_t(a):
        cp = remote(cots.at[1, a], cots.at[1, a], z_send.at[0], t_recv.at[a], hop[0])
        when(third, cp.wait_recv)

    def wait_x(k, d, cond):
        block = cots.at[2 * k, slot(d) * NJ : (slot(d) + 1) * NJ]
        cp = remote(block, block, z_send.at[0], c_recv.at[k, slot(d)], hop[0])
        when(cond, cp.wait_recv)

    def own():
        for d in (0, 1):
            send_z(0, 0, d)
        for i in (1, 2, 3):
            send(remote(gp.at[mine], gp.at[mine], y_send, p_recv.at[mine], at(jj=order[i])))
        send_x(mine, 0, 0)

    to_line = {
        (): (False, False, False),
        (3,): (j == 3, (j == 0) | (j == 3), j == 0),
        (2, 3): (j >= 2, (j == 0) | (j == 3), True),
        (1, 2, 3): (True, True, True),
    }[RING]

    def t0():
        wait_t(mine)
        for i, cond in zip((1, 2, 3), to_line):
            if cond is not False:
                cp = remote(cots.at[1, mine], cots.at[1, mine], yt_send.at[i], t_recv.at[mine], at(jj=order[i]))
                send(cp, third & cond)

    def y(i):
        a = chunk(0, i)
        wait_p(a)
        for d in (0, 1):
            send_z(0, i, d)
        send_x(a, 0, i)

    def ty(i):
        if i in RING:
            wait_t(chunk(0, i))
            for d in (0, 1):
                send_zt(0, i, d)

    def zp(r, i):
        for d in (0, 1):
            if r == 4 and (i < 2) != (d == 0):
                continue
            a = chunk(here(r, d), i)
            wait_p(a)
            if r < 3 or (r == 3 and (i < 2) == (d == 0)):
                send_z(r, i, d)
            send_x(a, here(r, d), i)

    def zt(r, i):
        for d in (0, 1):
            if i not in RING or (r == 4 and (i == 2) != (d == 0)):
                continue
            wait_t(chunk(here(r, d), i))
            if r < 3 or (r == 3 and (i == 2) == (d == 0)):
                send_zt(r, i, d)

    def setup():
        for cp, cond in loads:
            when(cond, cp.wait)
        wtail[...] = jnp.zeros_like(wtail)
        for k in range(NX + 1):
            wtail[k, 0:TAIL, 0:FEATS] = weight[k, MAIN:D, :]
            wtail[k, TAIL : 2 * TAIL, FEATS : 2 * FEATS] = weight[k, MAIN:D, :]
        for t in range(NX):
            @pl.when(t < x)
            def _():
                dec_out[t] = jnp.zeros((D, FEATS), BF16)

    def times(data, k):
        both = jnp.concatenate(
            [data[:, :, 0:MAIN].reshape(HALF, MAIN), data[:, :, MAIN : 2 * MAIN].reshape(HALF, MAIN)], axis=0
        )
        main = nn(both, weight[k, 0:MAIN, :])
        tails = nn(data[:, :, 2 * MAIN :].reshape(HALF, 2 * TAIL), wtail[k])
        return main[0:HALF] + tails[:, 0:FEATS], main[HALF:] + tails[:, FEATS:]

    def pre(d):
        s = slot(d)
        part[0, s, 0], part[0, s, 1] = times(gp[s * NJ : (s + 1) * NJ, 0], 0)
        sum1(0, s).start()

    def act(d):
        wait_x(0, d, x <= 2)
        for i in range(NJ):
            if i not in RING and (d or i):
                wait_t(chunk(d, i))
        wait_x(1, d, x == 0)
        s = slot(d)
        ch = slice(s * NJ, (s + 1) * NJ)
        part[1, s, 0], part[1, s, 1] = times(gp[ch, 1], 1)
        for k, cond in enumerate((x <= 2, x <= 1, x == 0)):
            @pl.when(cond)
            def _():
                a, b = times(cots[k, ch], k + 2)
                part[1, s, 0] += a
                part[1, s, 1] += b
        sum1(1, s).start()

    def sum1(k, s):
        return remote(part.at[k, s, 1 - c], r1.at[k, s], r_send.at[0, k], r_recv.at[0, k, s], core_peer)

    def sum2(k, s):
        return remote(s2.at[k, s], r2.at[k, s], r_send.at[1, k], r_recv.at[1, k, s], far_peer)

    def sum3(k, s, half):
        block = af.at[k, half, s * HALF : (s + 1) * HALF]
        return remote(block, block, r_send.at[2, k], r_recv.at[2, k, s], core_peer)

    def red2(k, d):
        s = slot(d)
        sum1(k, s).wait_recv()
        s2[k, s] = (part[k, s, c] + r1[k, s]).astype(BF16)
        sum2(k, s).start()

    def red3(k, d):
        s = slot(d)
        sum2(k, s).wait_recv()
        total = s2[k, s].astype(F32) + r2[k, s].astype(F32)
        if k == 0:
            total = total + bias[...]
        gate = active[pl.ds(zi(d) * NJ, NJ)].reshape(HALF, FEATS).astype(F32)
        af[k, c, s * HALF : (s + 1) * HALF, :] = (total * gate).astype(BF16)
        sum3(k, s, c).start()

    def red4(k, d):
        s = slot(d)
        sum3(k, s, 1 - c).wait_recv()
        if k == 1:
            for h in (0, 1):
                fg_out[pl.ds(zi(d) * NJ, NJ), h] = af[1, h, s * HALF : (s + 1) * HALF].reshape(NJ, SUB, FEATS)

    def grads(data, k):
        a, b, n = af[k, 0], af[k, 1], NZ * HALF
        main = tn(data[:, :, 0:MAIN].reshape(n, MAIN), a) + tn(data[:, :, MAIN : 2 * MAIN].reshape(n, MAIN), b)
        tails = data[:, :, 2 * MAIN :].reshape(n, 2 * TAIL)
        return main.astype(BF16), (tn(tails, a)[0:TAIL] + tn(tails, b)[TAIL:]).astype(BF16)

    def dec():
        for k in range(NX):
            @pl.when(x + k < NX)
            def _():
                dec_out[x + k, 0:MAIN], dec_out[x + k, MAIN:D] = grads(cots[k - 1] if k else gp[:, 1], 0)

    def enc():
        enc_out[0:MAIN], enc_out[MAIN:D] = grads(gp[:, 0], 1)
        bias_out[...] = sum(jnp.sum(af[1, h].astype(F32), axis=0, keepdims=True) for h in (0, 1))

    def wait_sent():
        def done(ref, sem, cond=None):
            when(cond, remote(ref, ref, sem, p_recv.at[0], hop[0]).wait_send)

        sent = NZ // 2 * NJ - NJ // 2
        for d in (0, 1):
            done(gp.at[0:sent], z_send.at[d])
            n = sum(3 + ((i == 2) == (d == 0)) for i in RING)
            if n:
                done(cots.at[1, 0:n], zt_send.at[d], third)
        done(gp.at[0 : NJ - 1], y_send)
        for i, cond in zip((1, 2, 3), to_line):
            if cond is not False:
                done(cots.at[1, 0], yt_send.at[i], third & cond)
        done(cots.at[0], x_send.at[0], x >= 1)
        done(cots.at[0], x_send.at[1], x == 3)
        direct = CHUNKS - NZ * len(RING)
        done(cots.at[1, 0:direct], x_send.at[2], x >= 2)

    own()
    y(1), zp(1, 0), y(2), zp(1, 1), y(3), t0(), ty(1)
    setup()
    zp(1, 2), ty(2), pre(0), zp(1, 3), ty(3), zp(2, 0), zp(2, 1), act(0), pre(-1)
    zt(1, 1), zt(1, 2), red2(0, 0), pre(1), zp(2, 2), zt(1, 3), act(-1), red2(1, 0), zp(2, 3), red2(0, -1), act(1)
    red2(0, 1), zp(3, 0), zt(2, 1), pre(-2), zt(2, 2), red2(1, -1), pre(2), zp(3, 1), red2(1, 1), zt(2, 3)
    red2(0, -2), act(-2), zp(3, 2), red2(0, 2), act(2), zp(3, 3), red2(1, -2), zt(3, 1), pre(-3), zt(3, 2), red2(1, 2)
    pre(3), red2(0, -3), zt(3, 3), zp(4, 0), zp(4, 2), red2(0, 3), act(-3), zp(4, 1), zp(4, 3), pre(4), red2(1, -3)
    act(3), red2(0, 4), zt(4, 1), zt(4, 2), red2(1, 3), zt(4, 3), act(4)
    for d in (0, -1, 1):
        red3(0, d)
    red2(1, 4)
    for d in (-2, 2, -3, 3):
        red3(0, d)
    for d in (0, -1, 1, -2, 2):
        red3(1, d)
    red3(0, 4)
    wait_sent()
    for d in range(-3, 5):
        red4(0, d)
    dec()
    for d in (-3, 3, 4):
        red3(1, d)
    for d in range(-3, 5):
        red4(1, d)
    enc()
    for k in (0, 1):
        for n, ref in enumerate((r1.at[k], s2.at[k], af.at[k, 0])):
            remote(ref, ref, r_send.at[n, k], p_recv.at[0], hop[0]).wait_send()


def write_kernel(dec, enc, bias, fg, dec_out, enc_out, bias_out, fg_out, sem):
    copies = [
        pltpu.make_async_copy(dec, dec_out, sem.at[0]),
        pltpu.make_async_copy(enc, enc_out, sem.at[1]),
        pltpu.make_async_copy(bias, bias_out, sem.at[2]),
        pltpu.make_async_copy(fg, fg_out, sem.at[3]),
    ]
    for cp in copies:
        cp.start()
    for cp in copies:
        cp.wait()


def local(residuals, cotangent, enc_weight, enc_bias, dec_weight, active):
    vmem, hbm = pl.BlockSpec(memory_space=pltpu.VMEM), pl.BlockSpec(memory_space=pltpu.HBM)
    dma = pltpu.SemaphoreType.DMA
    outs = [((NX, D, FEATS), BF16), ((D, FEATS), BF16), ((1, FEATS), F32), ((CHUNKS, 2, SUB, FEATS), BF16)]
    held = pl.pallas_call(
        gather_kernel,
        out_shape=tuple(pltpu.VMEM(shape, dtype) for shape, dtype in outs),
        in_specs=[hbm] * 6,
        out_specs=(vmem,) * 4,
        scratch_shapes=[
            pltpu.VMEM((2, TOK, D), BF16),
            pltpu.VMEM((CHUNKS, 2, SUB, WIDE), BF16),
            pltpu.VMEM((3, CHUNKS, SUB, WIDE), BF16),
            pltpu.VMEM((NX + 1, D, FEATS), BF16),
            pltpu.VMEM((NX + 1, 2 * TAIL, 2 * FEATS), BF16),
            pltpu.VMEM((1, FEATS), F32),
            pltpu.VMEM((CHUNKS, SUB, FEATS), jnp.int32),
            pltpu.VMEM((2, NZ, 2, HALF, FEATS), F32),
            pltpu.VMEM((2, NZ, HALF, FEATS), F32),
            pltpu.VMEM((2, NZ, HALF, FEATS), BF16),
            pltpu.VMEM((2, NZ, HALF, FEATS), BF16),
            pltpu.VMEM((2, 2, NZ * HALF, FEATS), BF16),
            dma((5 + NX,)),
            dma((CHUNKS,)),
            dma((2, NZ)),
            dma((CHUNKS,)),
            dma((2,)),
            dma((2,)),
            dma,
            dma((NJ,)),
            dma((3,)),
            dma((3, 2, NZ)),
            dma((3, 2)),
        ],
        compiler_params=pltpu.CompilerParams(collective_id=0, has_side_effects=True, vmem_limit_bytes=62 * 2**20),
    )(
        residuals,
        cotangent,
        enc_bias,
        enc_weight,
        jnp.swapaxes(dec_weight, 2, 3),
        active.reshape(CHUNKS, 2, SUB, FEATS),
    )
    dec_grad, enc_grad, bias_grad, feat_grad = pl.pallas_call(
        write_kernel,
        out_shape=tuple(jax.ShapeDtypeStruct(shape, dtype) for shape, dtype in outs),
        in_specs=[vmem] * 4,
        out_specs=(hbm,) * 4,
        scratch_shapes=[dma((4,))],
        compiler_params=pltpu.CompilerParams(vmem_limit_bytes=8 * 2**20),
    )(*held)
    return (
        jnp.swapaxes(dec_grad, 1, 2)[None],
        enc_grad[None],
        bias_grad,
        feat_grad.reshape(1, CHUNKS * TOK, FEATS),
    )


def solution(mesh):
    in_specs = (
        P("layer", "feat", "width"),
        P("layer", "feat", "width"),
        P("layer", "width", "feat"),
        P("layer", "feat"),
        P("layer", None, "feat", "width"),
        P("layer", None, "feat"),
    )
    out_specs = (
        P("layer", None, "feat", "width"),
        P("layer", "width", "feat"),
        P("layer", "feat"),
        P("layer", None, "feat"),
    )
    return jax.shard_map(local, mesh=mesh, in_specs=in_specs, out_specs=out_specs, check_vma=False)
```

time: 73.9 us -> 67.2 us (0.909)
  Pallas kernels: 72.9 us -> 66.5 us
    pallas_call x1, Pallas kernels: 71.6 us -> 65.1 us  [local(): pl.pallas_call(gather_kernel, out_shape=tuple((pltpu.VMEM(shape, dtype) f...]
where the time goes in v4:
time: 67.2 us; the launch traced here: 67.1 us
  Pallas kernels  66.5 us (99%)
    pallas_call x1, Pallas kernels, local(): pl.pallas_call(gather_kernel, out_shape=tuple((pltpu.VMEM(shape, dtype) f...  65.1 us

profile of v4, /device:TPU:1, one launch (start us, length us, event | category | flops | bytes accessed | tf_op | source)
XLA Modules:
  0.0 67.1 jit_solution(17304524583130145256)
XLA Ops:
  0.6 65.1 %shard_map.93 = (bf16[4,576,256]{2,1,0:T(8,128)(2,1)S(1)}, bf16[576,256]{1,0:T(8,128)(2,1)S(1)}, f32[1,256]{1,0:T(1,128)S(1)}, bf16[32,2,16,256]{3,2,1,0:T(8,128)(2,1)S(1)}) custom-call(bf16[1,32,576]{2,1,0:T(8,128)(2,1)} %resid_hbm.1, bf16[1,32,576]{2,1,0:T(8,128)(2,1)} %cot_hbm.1, f32[1,256]{1,0:T(1,128)} %bias_hbm.1, bf16[1,576,256]{2,1,0:T(8,128)(2,1)} %encw_hbm.1, ...), custom_call_target="tpu_custom_call" | custom-call | tf_op jit(solution)/shard_map/pallas_call | solution.py:353
  65.8 1.3 %shard_map.94 = (bf16[4,576,256]{2,1,0:T(8,128)(2,1)}, bf16[576,256]{1,0:T(8,128)(2,1)}, f32[1,256]{1,0:T(1,128)}, bf16[32,2,16,256]{3,2,1,0:T(8,128)(2,1)}) custom-call(bf16[4,576,256]{2,1,0:T(8,128)(2,1)S(1)} %get-tuple-element.12.dec, bf16[576,256]{1,0:T(8,128)(2,1)S(1)} %get-tuple-element.13.enc, f32[1,256]{1,0:T(1,128)S(1)} %get-tuple-element.14.bias, ...), custom_call_target="tpu_custom_call" | custom-call | tf_op jit(solution)/shard_map/pallas_call | solution.py:392

commit v5 on v4

--- a/solution.py
+++ b/solution.py
@@ -18,6 +18,7 @@
 WIDE = 2 * D
 FEATS = 256
 CHUNKS = NZ * NJ
+LAST = NZ - 1
 RING = (1, 2, 3)
 
 
@@ -68,17 +69,17 @@
         else:
             pl.when(cond)(fn)
 
-    barrier = pltpu.get_barrier_semaphore()
-    peers = [core_peer, far_peer, hop[0], hop[1], at(1), at(2), at(3)] + [at(jj=order[i]) for i in (1, 2, 3)]
-    for dev in peers:
-        pl.semaphore_signal(barrier, inc=1, device_id=dev, device_id_type=MESH)
-
     first = [
         pltpu.make_async_copy(resid_hbm.at[0], raw.at[0], loc_sem.at[0]),
         pltpu.make_async_copy(cot_hbm.at[0], raw.at[1], loc_sem.at[1]),
     ]
     for cp in first:
         cp.start()
+    barrier = pltpu.get_barrier_semaphore()
+    peers = [core_peer, far_peer, hop[0], hop[1], at(1), at(2), at(3)] + [at(jj=order[i]) for i in (1, 2, 3)]
+    for dev in peers:
+        pl.semaphore_signal(barrier, inc=1, device_id=dev, device_id_type=MESH)
+
     loads = [
         (pltpu.make_async_copy(encw_hbm.at[0], weight.at[0], loc_sem.at[2]), None),
         (pltpu.make_async_copy(active_hbm.at[:, c], active, loc_sem.at[3]), None),
@@ -121,11 +122,13 @@
         a, b = chunk(here(r, d), i), chunk(next_d(r, d), i)
         send(remote(cots.at[1, a], cots.at[1, b], zt_send.at[d], t_recv.at[b], hop[d]), third)
 
+    straight = lambda d, i: i not in RING or d == 4
+
     def send_x(a, d, i):
         own, s = gp.at[a, 1], slot(d)
         send(remote(own, cots.at[0, a], x_send.at[0], c_recv.at[0, s], at(3)), x >= 1)
         send(remote(own, cots.at[2, a], x_send.at[1], c_recv.at[1, s], at(1)), x == 3)
-        if i not in RING or (d == 0 and i == 0):
+        if straight(d, i) or (d == 0 and i == 0):
             send(remote(own, cots.at[1, a], x_send.at[2], t_recv.at[a], at(2)), x >= 2)
 
     def wait_p(a):
@@ -185,12 +188,11 @@
             send_x(a, here(r, d), i)
 
     def zt(r, i):
-        for d in (0, 1):
-            if i not in RING or (r == 4 and (i == 2) != (d == 0)):
-                continue
-            wait_t(chunk(here(r, d), i))
-            if r < 3 or (r == 3 and (i == 2) == (d == 0)):
-                send_zt(r, i, d)
+        if i in RING:
+            for d in (0, 1):
+                wait_t(chunk(here(r, d), i))
+                if r < 3:
+                    send_zt(r, i, d)
 
     def setup():
         for cp, cond in loads:
@@ -220,7 +222,7 @@
     def act(d):
         wait_x(0, d, x <= 2)
         for i in range(NJ):
-            if i not in RING and (d or i):
+            if straight(d, i) and (d or i):
                 wait_t(chunk(d, i))
         wait_x(1, d, x == 0)
         s = slot(d)
@@ -290,31 +292,29 @@
         sent = NZ // 2 * NJ - NJ // 2
         for d in (0, 1):
             done(gp.at[0:sent], z_send.at[d])
-            n = sum(3 + ((i == 2) == (d == 0)) for i in RING)
-            if n:
-                done(cots.at[1, 0:n], zt_send.at[d], third)
+            done(cots.at[1, 0 : 3 * len(RING)], zt_send.at[d], third)
         done(gp.at[0 : NJ - 1], y_send)
         for i, cond in zip((1, 2, 3), to_line):
             if cond is not False:
                 done(cots.at[1, 0], yt_send.at[i], third & cond)
         done(cots.at[0], x_send.at[0], x >= 1)
         done(cots.at[0], x_send.at[1], x == 3)
-        direct = CHUNKS - NZ * len(RING)
+        direct = CHUNKS - LAST * len(RING)
         done(cots.at[1, 0:direct], x_send.at[2], x >= 2)
 
     own()
-    y(1), zp(1, 0), y(2), zp(1, 1), y(3), t0(), ty(1)
+    y(1), zp(1, 0), y(2), zp(1, 1), y(3), t0()
     setup()
-    zp(1, 2), ty(2), pre(0), zp(1, 3), ty(3), zp(2, 0), zp(2, 1), act(0), pre(-1)
-    zt(1, 1), zt(1, 2), red2(0, 0), pre(1), zp(2, 2), zt(1, 3), act(-1), red2(1, 0), zp(2, 3), red2(0, -1), act(1)
-    red2(0, 1), zp(3, 0), zt(2, 1), pre(-2), zt(2, 2), red2(1, -1), pre(2), zp(3, 1), red2(1, 1), zt(2, 3)
-    red2(0, -2), act(-2), zp(3, 2), red2(0, 2), act(2), zp(3, 3), red2(1, -2), zt(3, 1), pre(-3), zt(3, 2), red2(1, 2)
-    pre(3), red2(0, -3), zt(3, 3), zp(4, 0), zp(4, 2), red2(0, 3), act(-3), zp(4, 1), zp(4, 3), pre(4), red2(1, -3)
-    act(3), red2(0, 4), zt(4, 1), zt(4, 2), red2(1, 3), zt(4, 3), act(4)
-    for d in (0, -1, 1):
+    zp(1, 2), pre(0), ty(1), zp(1, 3), ty(2), zp(2, 0), ty(3), zp(2, 1), pre(-1), act(0), pre(1)
+    zt(1, 1), red2(0, 0), zp(2, 2), zt(1, 2), red2(0, -1), red2(0, 1), zp(2, 3), red2(1, 0), zt(1, 3)
+    pre(-2), pre(2), zp(3, 0), act(-1), zt(2, 1), zp(3, 1), act(1), red2(0, -2), zt(2, 2), red2(0, 2), zp(3, 2)
+    red2(1, -1), zt(2, 3), red2(1, 1), zp(3, 3), pre(-3), pre(3), act(-2), zt(3, 1), zp(4, 0), zp(4, 2), red2(0, -3)
+    act(2), red2(0, 3), zp(4, 1), zp(4, 3), pre(4), red2(1, -2), zt(3, 2), red2(1, 2), zt(3, 3), act(-3)
+    red2(0, 4), act(3), red2(1, -3), act(4), red2(1, 3)
+    for d in (0, -1, 1, -2, 2):
         red3(0, d)
     red2(1, 4)
-    for d in (-2, 2, -3, 3):
+    for d in (-3, 3):
         red3(0, d)
     for d in (0, -1, 1, -2, 2):
         red3(1, d)

time: 67.2 us -> 66 us (0.982)
  Pallas kernels: 66.5 us -> 65 us
    pallas_call x1, Pallas kernels: 65.1 us -> 63.7 us  [local(): pl.pallas_call(gather_kernel, out_shape=tuple((pltpu.VMEM(shape, dtype) f...]
where the time goes in v5:
time: 66 us; the launch traced here: 65.6 us
  Pallas kernels  65 us (98%)
    pallas_call x1, Pallas kernels, local(): pl.pallas_call(gather_kernel, out_shape=tuple((pltpu.VMEM(shape, dtype) f...  63.7 us
    pallas_call x1, Pallas kernels, local(): pl.pallas_call(write_kernel, out_shape=tuple((jax.ShapeDtypeStruct(shape,...  1.32 us

profile of v5, /device:TPU:1, one launch (start us, length us, event | category | flops | bytes accessed | tf_op | source)
XLA Modules:
  0.0 65.6 jit_solution(15857478889765483974)
XLA Ops:
  0.6 63.7 %shard_map.93 = (bf16[4,576,256]{2,1,0:T(8,128)(2,1)S(1)}, bf16[576,256]{1,0:T(8,128)(2,1)S(1)}, f32[1,256]{1,0:T(1,128)S(1)}, bf16[32,2,16,256]{3,2,1,0:T(8,128)(2,1)S(1)}) custom-call(bf16[1,32,576]{2,1,0:T(8,128)(2,1)} %resid_hbm.1, bf16[1,32,576]{2,1,0:T(8,128)(2,1)} %cot_hbm.1, f32[1,256]{1,0:T(1,128)} %bias_hbm.1, bf16[1,576,256]{2,1,0:T(8,128)(2,1)} %encw_hbm.1, ...), custom_call_target="tpu_custom_call" | custom-call | tf_op jit(solution)/shard_map/pallas_call | solution.py:353
  64.3 1.3 %shard_map.94 = (bf16[4,576,256]{2,1,0:T(8,128)(2,1)}, bf16[576,256]{1,0:T(8,128)(2,1)}, f32[1,256]{1,0:T(1,128)}, bf16[32,2,16,256]{3,2,1,0:T(8,128)(2,1)}) custom-call(bf16[4,576,256]{2,1,0:T(8,128)(2,1)S(1)} %get-tuple-element.12.dec, bf16[576,256]{1,0:T(8,128)(2,1)S(1)} %get-tuple-element.13.enc, f32[1,256]{1,0:T(1,128)S(1)} %get-tuple-element.14.bias, ...), custom_call_target="tpu_custom_call" | custom-call | tf_op jit(solution)/shard_map/pallas_call | solution.py:392

commit v6 on v5

--- a/solution.py
+++ b/solution.py
@@ -259,15 +259,17 @@
         if k == 0:
             total = total + bias[...]
         gate = active[pl.ds(zi(d) * NJ, NJ)].reshape(HALF, FEATS).astype(F32)
-        af[k, c, s * HALF : (s + 1) * HALF, :] = (total * gate).astype(BF16)
+        done = (total * gate).astype(BF16)
+        af[k, c, s * HALF : (s + 1) * HALF, :] = done
         sum3(k, s, c).start()
+        if k == 1:
+            fg_out[pl.ds(zi(d) * NJ, NJ), c] = done.reshape(NJ, SUB, FEATS)
 
     def red4(k, d):
         s = slot(d)
         sum3(k, s, 1 - c).wait_recv()
         if k == 1:
-            for h in (0, 1):
-                fg_out[pl.ds(zi(d) * NJ, NJ), h] = af[1, h, s * HALF : (s + 1) * HALF].reshape(NJ, SUB, FEATS)
+            fg_out[pl.ds(zi(d) * NJ, NJ), 1 - c] = af[1, 1 - c, s * HALF : (s + 1) * HALF].reshape(NJ, SUB, FEATS)
 
     def grads(data, k):
         a, b, n = af[k, 0], af[k, 1], NZ * HALF
@@ -309,8 +311,8 @@
     zt(1, 1), red2(0, 0), zp(2, 2), zt(1, 2), red2(0, -1), red2(0, 1), zp(2, 3), red2(1, 0), zt(1, 3)
     pre(-2), pre(2), zp(3, 0), act(-1), zt(2, 1), zp(3, 1), act(1), red2(0, -2), zt(2, 2), red2(0, 2), zp(3, 2)
     red2(1, -1), zt(2, 3), red2(1, 1), zp(3, 3), pre(-3), pre(3), act(-2), zt(3, 1), zp(4, 0), zp(4, 2), red2(0, -3)
-    act(2), red2(0, 3), zp(4, 1), zp(4, 3), pre(4), red2(1, -2), zt(3, 2), red2(1, 2), zt(3, 3), act(-3)
-    red2(0, 4), act(3), red2(1, -3), act(4), red2(1, 3)
+    act(2), red2(0, 3), zp(4, 1), zp(4, 3), pre(4), red2(1, -2), zt(3, 2), red2(1, 2), zt(3, 3), red2(0, 4)
+    act(-3), act(3), red2(1, -3), act(4), red2(1, 3)
     for d in (0, -1, 1, -2, 2):
         red3(0, d)
     red2(1, 4)

time: 66 us -> 66.1 us (level)
  no operation moved by 1% of the time
where the time goes in v6:
time: 66.1 us; the launch traced here: 66 us
  Pallas kernels  65.4 us (99%)
    pallas_call x1, Pallas kernels, local(): pl.pallas_call(gather_kernel, out_shape=tuple((pltpu.VMEM(shape, dtype) f...  64 us

profile of v6, /device:TPU:1, one launch (start us, length us, event | category | flops | bytes accessed | tf_op | source)
XLA Modules:
  0.0 66.0 jit_solution(12342701853763893747)
XLA Ops:
  0.6 64.0 %shard_map.93 = (bf16[4,576,256]{2,1,0:T(8,128)(2,1)S(1)}, bf16[576,256]{1,0:T(8,128)(2,1)S(1)}, f32[1,256]{1,0:T(1,128)S(1)}, bf16[32,2,16,256]{3,2,1,0:T(8,128)(2,1)S(1)}) custom-call(bf16[1,32,576]{2,1,0:T(8,128)(2,1)} %resid_hbm.1, bf16[1,32,576]{2,1,0:T(8,128)(2,1)} %cot_hbm.1, f32[1,256]{1,0:T(1,128)} %bias_hbm.1, bf16[1,576,256]{2,1,0:T(8,128)(2,1)} %encw_hbm.1, ...), custom_call_target="tpu_custom_call" | custom-call | tf_op jit(solution)/shard_map/pallas_call | solution.py:355
  64.7 1.3 %shard_map.94 = (bf16[4,576,256]{2,1,0:T(8,128)(2,1)}, bf16[576,256]{1,0:T(8,128)(2,1)}, f32[1,256]{1,0:T(1,128)}, bf16[32,2,16,256]{3,2,1,0:T(8,128)(2,1)}) custom-call(bf16[4,576,256]{2,1,0:T(8,128)(2,1)S(1)} %get-tuple-element.12.dec, bf16[576,256]{1,0:T(8,128)(2,1)S(1)} %get-tuple-element.13.enc, f32[1,256]{1,0:T(1,128)S(1)} %get-tuple-element.14.bias, ...), custom_call_target="tpu_custom_call" | custom-call | tf_op jit(solution)/shard_map/pallas_call | solution.py:394
